TPU v7x, 32 devices: a whole 2x2x4 slice. The times are simulated.
32 devices in a mesh: crops: 2 (over y), xy: 4 (over z), gz: 2 (over x), lab: 2 (over core).
Axes of the slice: x: 2, y: 2, z: 4, core: 2. Of those that a mesh axis runs over, the one named last changes fastest.
Arguments:
- image: bfloat16 [16, 32, 64, 128], P('lab', ('crops', 'xy'), 'gz'), parts along dimension 1, may hold values from -6 to 6
- filt: bfloat16 [3, 16, 3, 3, 3], replicated, may hold values from -0.3125 to 0.3125
- planted_colours: int32 [32, 64, 128], P(('crops', 'xy'), 'gz'), parts along dimension 0, may hold values from 0 to 63
- likelihoods: float32 [8, 32, 64, 128], P('lab', ('crops', 'xy'), 'gz'), parts along dimension 1, may hold values from 0 to 1
- loss_slope: float32 [8, 32, 64, 128], P('lab', ('crops', 'xy'), 'gz'), parts along dimension 1, may hold values from -5.25 to 5.25
Outputs:
- grad_image: bfloat16 [16, 32, 64, 128], P('lab', ('crops', 'xy'), 'gz'), parts along dimension 1
- grad_filter: float32 [6, 16, 3, 3, 3], P('crops', 'lab'), parts along dimension 0
There are 2 independent parts, one for each index of `crops`. A program takes and returns all parts, laid end to end along the dimension named above; an argument that names none is the same for every part. Nothing has to cross between parts.
Inputs may be any that keep to these rules, and one draw needn't show every extreme that they name: `planted_colours`: A value below 8 marks a seed of that colour; any other value marks an unseeded cell.
All inputs are finite; a program needn't handle non-finite values.
Results may differ from a plain program's by a relative error of at most 0.015.
Values may be sent and summed in bfloat16 or wider, within the bound.
No kernel may reach another device: no remote copies, remote signals or barrier semaphores. Data moves between devices by JAX's collectives and lax.ppermute only.
A program may use at most 64 MiB of HBM per device.

v0:
```python
import jax
import jax.numpy as jnp
from jax import lax
from jax.sharding import PartitionSpec as P

ITERS = 3


def with_halo(cells, sides, width):
    for axis, dim in sides:
        count = lax.axis_size(axis)
        ends = count - 1
        head = lax.slice_in_dim(cells, 0, width, axis=dim)
        tail = lax.slice_in_dim(cells, cells.shape[dim] - width, cells.shape[dim], axis=dim)
        cells = jnp.concatenate(
            [
                lax.ppermute(tail, axis, [(i, (i + 1) % count) for i in range(ends)]),
                cells,
                lax.ppermute(head, axis, [((i + 1) % count, i) for i in range(ends)]),
            ],
            axis=dim,
        )
    return cells


def passed_along(block, axis, distance):
    devices = range(lax.axis_size(axis))
    route = [(i - distance, i) for i in devices if i - distance in devices]
    return lax.ppermute(block, axis, route)


def offsets():
    return [
        (first, second, third) for first in range(3) for second in range(3) for third in range(3)
    ]


def correlate(weights, wide, rows_x, rows_z, rows_y):
    grand_quantity = jnp.zeros((weights.shape[0], rows_x, rows_z, rows_y), jnp.float32)
    for first, second, third in offsets():
        window = wide[:, first : first + rows_x, second : second + rows_z, third : third + rows_y]
        grand_quantity = grand_quantity + jnp.einsum(
            "dc,cxzy->dxzy",
            weights[:, :, first, second, third],
            window,
            preferred_element_type=jnp.float32,
        )
    return grand_quantity


def squares(remainder_grid):
    return lax.psum(jnp.sum(remainder_grid * remainder_grid, axis=(1, 2, 3)), ("xy", "gz"))[
        :, None, None, None
    ]


def local(image, filt, planted_colours, likelihoods, loss_slope):
    channels_here = image.shape[0]
    labels_here = likelihoods.shape[0]
    rows_x, rows_z, rows_y = (likelihoods.shape[1], likelihoods.shape[2], likelihoods.shape[3])
    lab_index = lax.axis_index("lab")
    own_filt = lax.dynamic_slice_in_dim(filt, lab_index * channels_here, channels_here, 1)
    image_edge = with_halo(image, (("xy", 1), ("gz", 2)), 1)
    own_wide = jnp.pad(image_edge, ((0, 0), (0, 0), (0, 0), (1, 1)))
    logits = lax.psum(
        correlate(own_filt, own_wide, rows_x, rows_z, rows_y).astype(jnp.bfloat16), "lab"
    ).astype(jnp.float32)
    xy_index = lax.axis_index("xy")
    gz_index = lax.axis_index("gz")
    xy_count = lax.axis_size("xy")
    gz_count = lax.axis_size("gz")
    shape = (rows_x, rows_z, rows_y)
    along_x = jnp.arange(rows_x, dtype=jnp.int32) + xy_index * rows_x < rows_x * xy_count - 1
    along_z = jnp.arange(rows_z, dtype=jnp.int32) + gz_index * rows_z < rows_z * gz_count - 1
    along_y = jnp.arange(rows_y, dtype=jnp.int32) < rows_y - 1
    edge_valid = jnp.stack(
        [
            jnp.broadcast_to(along_x[:, None, None], shape),
            jnp.broadcast_to(along_z[None, :, None], shape),
            jnp.broadcast_to(along_y[None, None, :], shape),
        ]
    ).astype(jnp.float32)
    squashed = jax.nn.sigmoid(logits)
    weight = (0.05 + squashed) * edge_valid
    below_x = passed_along(weight[0, -1:], "xy", 1)
    lower_x = jnp.concatenate([below_x, weight[0, :-1]], axis=0)
    below_z = passed_along(weight[1, :, -1:], "gz", 1)
    lower_z = jnp.concatenate([below_z, weight[1, :, :-1]], axis=1)
    lower_y = jnp.concatenate(
        [jnp.zeros((rows_x, rows_z, 1), jnp.float32), weight[2, :, :, :-1]], axis=2
    )
    class_count_overall = labels_here * lax.axis_size("lab")
    free_cell_flags = (planted_colours >= class_count_overall).astype(jnp.float32)[None]
    colours = lab_index * labels_here + jnp.arange(labels_here, dtype=jnp.int32)
    class_membership = (planted_colours[None] == colours[:, None, None, None]).astype(jnp.float32)
    entire_grid_state = free_cell_flags * likelihoods + class_membership
    adjoint = jnp.zeros_like(likelihoods)
    remainder_grid = free_cell_flags * loss_slope
    direction = remainder_grid
    norm_now = squares(remainder_grid)
    for count in range(ITERS):
        extended = with_halo(direction.astype(jnp.bfloat16), (("xy", 1), ("gz", 2)), 1).astype(
            direction.dtype
        )
        zeros_y = jnp.zeros(direction.shape[:3] + (1,), jnp.float32)
        upper_y = jnp.concatenate([direction[..., 1:], zeros_y], axis=3)
        under_y = jnp.concatenate([zeros_y, direction[..., :-1]], axis=3)
        grand_quantity = weight[0] * (direction - extended[:, 2:, 1:-1]) + lower_x * (
            direction - extended[:, :-2, 1:-1]
        )
        grand_quantity = (
            grand_quantity
            + weight[1] * (direction - extended[:, 1:-1, 2:])
            + lower_z * (direction - extended[:, 1:-1, :-2])
        )
        grand_quantity = (
            grand_quantity + weight[2] * (direction - upper_y) + lower_y * (direction - under_y)
        )
        picture_pixels_flat = free_cell_flags * grand_quantity
        curve = lax.psum(jnp.sum(direction * picture_pixels_flat, axis=(1, 2, 3)), ("xy", "gz"))
        alpha = norm_now / curve[:, None, None, None]
        adjoint = adjoint + alpha * direction
        remainder_grid = remainder_grid - alpha * picture_pixels_flat
        norm_next = squares(remainder_grid)
        direction = remainder_grid + norm_next / norm_now * direction
        norm_now = norm_next
    field_pair = jnp.concatenate([adjoint, entire_grid_state], axis=0)
    above_x = passed_along(field_pair[:, :1].astype(jnp.bfloat16), "xy", -1).astype(jnp.float32)
    next_x = jnp.concatenate([field_pair[:, 1:], above_x], axis=1)
    above_z = passed_along(field_pair[:, :, :1], "gz", -1)
    next_z = jnp.concatenate([field_pair[:, :, 1:], above_z], axis=2)
    next_y = jnp.concatenate(
        [field_pair[..., 1:], jnp.zeros(field_pair.shape[:3] + (1,), jnp.float32)], axis=3
    )
    partial_grads = []
    for neighbour in (next_x, next_z, next_y):
        change = field_pair - neighbour
        partial_grads.append(-jnp.sum(change[:labels_here] * change[labels_here:], axis=0))
    edge_grad = lax.psum(jnp.stack(partial_grads), "lab")
    logit_grad = (edge_grad * squashed * (1.0 - squashed) * edge_valid).astype(jnp.bfloat16)
    grad_edge = with_halo(logit_grad, (("xy", 1), ("gz", 2)), 1)
    grad_wide = jnp.pad(grad_edge, ((0, 0), (0, 0), (0, 0), (1, 1)))
    grad_image = jnp.zeros((channels_here, rows_x, rows_z, rows_y), jnp.float32)
    filter_terms = []
    for first, second, third in offsets():
        window = grad_wide[
            :,
            2 - first : 2 - first + rows_x,
            2 - second : 2 - second + rows_z,
            2 - third : 2 - third + rows_y,
        ]
        grad_image = grad_image + jnp.einsum(
            "dc,dxzy->cxzy",
            own_filt[:, :, first, second, third],
            window,
            preferred_element_type=jnp.float32,
        )
        image_window = own_wide[
            :, first : first + rows_x, second : second + rows_z, third : third + rows_y
        ]
        filter_terms.append(
            jnp.einsum(
                "dxzy,cxzy->dc", logit_grad, image_window, preferred_element_type=jnp.float32
            )
        )
    filter_part = jnp.stack(filter_terms, axis=-1).reshape(3, channels_here, 3, 3, 3)
    grad_filter = lax.psum(filter_part, ("xy", "gz"))
    return (grad_image.astype(jnp.bfloat16), grad_filter)


def solution(mesh):
    return jax.shard_map(
        local,
        mesh=mesh,
        in_specs=(
            P("lab", ("crops", "xy"), "gz", None),
            P(),
            P(("crops", "xy"), "gz", None),
            P("lab", ("crops", "xy"), "gz", None),
            P("lab", ("crops", "xy"), "gz", None),
        ),
        out_specs=(P("lab", ("crops", "xy"), "gz", None), P("crops", "lab", None, None, None)),
        check_vma=False,
    )
```

profile of v0, /device:TPU:0, one launch (start us, length us, event | category | flops | bytes accessed | tf_op | source)
XLA Modules:
  0.0 312.0 jit_solution(1046695100650287679)
XLA Ops:
  7.2 1.2 copy.105
  8.4 1.3 collective-permute-start.1
  9.7 5.6 %collective-permute-start = (bf16[8,1,32,128]{3,0,2,1:T(8,128)(2,1)S(1)}, bf16[8,1,32,128]{3,0,2,1:T(8,128)(2,1)S(1)}, u32[]{:S(2)}, u32[]{:S(2)}) collective-permute-start(bf16[8,1,32,128]{3,0,2,1:T(8,128)(2,1)S(1)} %get-tuple-element.42), channel_id=1, source_target_pairs={{0,4},{4,8},{8,12},{1,5},{5,9},{9,13},{2,6},{6,10},{10,14},{3,7},{... | collective-permute-start | bytes 196616 | tf_op jit(solution)/shard_map/ppermute | solution.py:17
  15.3 0.8 compare_convert_fusion
  16.2 4.1 %collective-permute-start.4 = (bf16[4,1,32,128]{3,2,1,0:T(8,128)(2,1)S(1)}, bf16[4,1,32,128]{3,2,1,0:T(8,128)(2,1)S(1)}, u32[]{:S(2)}, u32[]{:S(2)}) collective-permute-start(bf16[4,1,32,128]{3,2,1,0:T(8,128)(2,1)S(1)} %get-tuple-element.59), channel_id=1, source_target_pairs={{0,4},{4,8},{8,12},{1,5},{5,9},{9,13},{2,6},{6,10},{10,14},{3,7},{... | collective-permute-start | bytes 98312 | tf_op jit(solution)/shard_map/ppermute | solution.py:17
  20.3 1.3 collective-permute-start.5
  21.6 0.8 fusion.315
  23.1 3.4 %collective-permute-start.2 = (bf16[8,6,1,128]{3,0,2,1:T(8,128)(2,1)S(1)}, bf16[8,6,1,128]{3,0,2,1:T(8,128)(2,1)S(1)}, u32[]{:S(2)}, u32[]{:S(2)}) collective-permute-start(bf16[8,6,1,128]{3,0,2,1:T(8,128)(2,1)S(1)} %get-tuple-element.30), channel_id=1, source_target_pairs={{0,2},{1,3},{4,6},{5,7},{8,10},{9,11},{12,14},{13,15},{16,18},{17,... | collective-permute-start | bytes 36872 | tf_op jit(solution)/shard_map/ppermute | solution.py:17
  26.5 1.3 collective-permute-start.3
  27.8 4.5 %collective-permute-start.6 = (bf16[4,6,1,128]{3,2,1,0:T(2,128)(2,1)S(1)}, bf16[4,6,1,128]{3,2,1,0:T(2,128)(2,1)S(1)}, u32[]{:S(2)}, u32[]{:S(2)}) collective-permute-start(bf16[4,6,1,128]{3,2,1,0:T(2,128)(2,1)S(1)} %get-tuple-element.51), channel_id=1, source_target_pairs={{0,2},{1,3},{4,6},{5,7},{8,10},{9,11},{12,14},{13,15},{16,18},{17,... | collective-permute-start | bytes 18440 | tf_op jit(solution)/shard_map/ppermute | solution.py:17
  32.4 1.3 collective-permute-start.7
  33.7 0.4 fusion.48
  40.5 0.4 copy-done.24
  41.3 0.9 fusion.16
  42.4 20.3 %all-reduce.14.cloned.1.call-done = bf16[3,4,32,128]{3,0,2,1:T(4,128)(2,1)} async-done(((bf16[3,4,32,128]{3,0,2,1:T(4,128)(2,1)}), bf16[3,4,32,128]{3,0,2,1:T(4,128)(2,1)}) %all-reduce.14.cloned.1.call-update) | async-done | bytes 98320 | tf_op jit(solution)/shard_map/psum | solution.py:65
  63.0 1.3 add_select_fusion
  64.4 3.6 %collective-permute-start.9 = (f32[4,1,128]{2,0,1:T(4,128)S(1)}, f32[4,1,128]{2,0,1:T(4,128)S(1)}, u32[]{:S(2)}, u32[]{:S(2)}) collective-permute-start(f32[4,1,128]{2,0,1:T(4,128)S(1)} %bitcast.468), channel_id=1, source_target_pairs={{0,2},{1,3},{4,6},{5,7},{8,10},{9,11},{12,14},{13,15},{16,18},{17,... | collective-permute-start | bytes 6152 | tf_op jit(solution)/shard_map/ppermute | solution.py:29
  68.4 3.4 %collective-permute-start.8 = (f32[1,32,128]{2,1,0:T(8,128)S(1)}, f32[1,32,128]{2,1,0:T(8,128)S(1)}, u32[]{:S(2)}, u32[]{:S(2)}) collective-permute-start(f32[1,32,128]{2,1,0:T(8,128)S(1)} %bitcast.466), channel_id=1, source_target_pairs={{0,4},{4,8},{8,12},{1,5},{5,9},{9,13},{2,6},{6,10},{10,14},{3,7},{... | collective-permute-start | bytes 49160 | tf_op jit(solution)/shard_map/ppermute | solution.py:29
  71.9 1.3 collective-permute-done.8
  73.2 0.4 multiply_reduce_fusion.3
  73.8 20.1 %all-reduce.10 = (f32[4]{0:T(128)S(1)}, f32[4]{0:T(128)S(1)}) all-reduce(f32[4]{0:T(128)S(1)} %get-tuple-element.13, f32[4]{0:T(128)S(1)} %get-tuple-element.12), channel_id=1, replica_groups=mesh['crops'=2,'xy'=4,'gz'=2,'lab'=2] {'xy','gz'}, use_global_device_ids=true, to_apply=%region_1.2 | all-reduce | flops 8 | bytes 64 | tf_op jit(solution)/shard_map/psum | solution.py:52
  94.1 17.2 %psum.66 = f32[4]{0:T(128)S(1)} all-reduce(f32[4]{0:T(128)S(1)} %get-tuple-element.22), channel_id=1, replica_groups=mesh['crops'=2,'xy'=4,'gz'=2,'lab'=2] {'xy','gz'}, use_global_device_ids=true, to_apply=%region_6.7 | all-reduce | flops 4 | bytes 32 | tf_op jit(solution)/shard_map/psum | solution.py:52
  111.4 0.5 copy-done.85
  112.0 1.3 collective-permute-start.10
  113.3 1.3 collective-permute-start.11
  114.9 4.2 %collective-permute-done.11 = bf16[4,1,32,128]{3,2,1,0:T(8,128)(2,1)S(1)} collective-permute-done((bf16[4,1,32,128]{3,2,1,0:T(8,128)(2,1)S(1)}, bf16[4,1,32,128]{3,2,1,0:T(8,128)(2,1)S(1)}, u32[]{:S(2)}, u32[]{:S(2)}) %collective-permute-start.11) | collective-permute-done | bytes 32800 | tf_op jit(solution)/shard_map/ppermute | solution.py:19
  119.1 3.8 %collective-permute-start.12 = (bf16[4,6,1,128]{3,2,1,0:T(2,128)(2,1)S(1)}, bf16[4,6,1,128]{3,2,1,0:T(2,128)(2,1)S(1)}, u32[]{:S(2)}, u32[]{:S(2)}) collective-permute-start(bf16[4,6,1,128]{3,2,1,0:T(2,128)(2,1)S(1)} %get-tuple-element.49), channel_id=1, source_target_pairs={{0,2},{1,3},{4,6},{5,7},{8,10},{9,11},{12,14},{13,15},{16,18},{17,... | collective-permute-start | bytes 18440 | tf_op jit(solution)/shard_map/ppermute | solution.py:17
  122.9 1.3 collective-permute-start.13
  124.4 4.1 %collective-permute-done.13 = bf16[4,6,1,128]{3,2,1,0:T(2,128)(2,1)S(1)} collective-permute-done((bf16[4,6,1,128]{3,2,1,0:T(2,128)(2,1)S(1)}, bf16[4,6,1,128]{3,2,1,0:T(2,128)(2,1)S(1)}, u32[]{:S(2)}, u32[]{:S(2)}) %collective-permute-start.13) | collective-permute-done | bytes 6176 | tf_op jit(solution)/shard_map/ppermute | solution.py:19
  128.7 0.9 multiply_reduce_fusion.1
  129.6 17.3 %psum.67 = f32[4]{0:T(128)S(1)} all-reduce(f32[4]{0:T(128)} %get-tuple-element.18), channel_id=1, replica_groups=mesh['crops'=2,'xy'=4,'gz'=2,'lab'=2] {'xy','gz'}, use_global_device_ids=true, to_apply=%region_8.9 | all-reduce | flops 4 | bytes 32 | tf_op jit(solution)/shard_map/psum | solution.py:120
  146.9 0.7 div.26
  147.7 19.1 %psum.68 = f32[4]{0:T(128)S(1)} all-reduce(f32[4]{0:T(128)S(1)} %multiply_reduce_fusion), channel_id=1, replica_groups=mesh['crops'=2,'xy'=4,'gz'=2,'lab'=2] {'xy','gz'}, use_global_device_ids=true, to_apply=%region_10.11 | all-reduce | flops 4 | bytes 32 | tf_op jit(solution)/shard_map/psum | solution.py:52
  166.8 0.6 copy-done.86
  167.4 0.7 div.27
  168.0 0.8 fusion.306
  168.8 1.3 collective-permute-start.14
  170.1 1.3 collective-permute-start.15
  171.7 4.2 %collective-permute-done.15 = bf16[4,1,32,128]{3,2,1,0:T(8,128)(2,1)S(1)} collective-permute-done((bf16[4,1,32,128]{3,2,1,0:T(8,128)(2,1)S(1)}, bf16[4,1,32,128]{3,2,1,0:T(8,128)(2,1)S(1)}, u32[]{:S(2)}, u32[]{:S(2)}) %collective-permute-start.15) | collective-permute-done | bytes 32800 | tf_op jit(solution)/shard_map/ppermute | solution.py:19
  176.0 2.0 collective-permute-start.16
  177.9 1.3 collective-permute-start.17
  179.4 4.1 %collective-permute-done.17 = bf16[4,6,1,128]{3,2,1,0:T(2,128)(2,1)S(1)} collective-permute-done((bf16[4,6,1,128]{3,2,1,0:T(2,128)(2,1)S(1)}, bf16[4,6,1,128]{3,2,1,0:T(2,128)(2,1)S(1)}, u32[]{:S(2)}, u32[]{:S(2)}) %collective-permute-start.17) | collective-permute-done | bytes 6176 | tf_op jit(solution)/shard_map/ppermute | solution.py:19
  183.7 0.4 fusion.71
  184.1 17.2 %psum.69 = f32[4]{0:T(128)S(1)} all-reduce(f32[4]{0:T(128)S(1)} %fusion.71), channel_id=1, replica_groups=mesh['crops'=2,'xy'=4,'gz'=2,'lab'=2] {'xy','gz'}, use_global_device_ids=true, to_apply=%region_12.13 | all-reduce | flops 4 | bytes 32 | tf_op jit(solution)/shard_map/psum | solution.py:120
  201.7 1.3 collective-permute-start.19
  203.0 1.5 collective-permute-start.18
  204.5 4.6 %collective-permute-done.18 = bf16[8,1,32,128]{3,2,1,0:T(8,128)(2,1)S(1)} collective-permute-done((bf16[8,1,32,128]{3,2,1,0:T(8,128)(2,1)S(1)}, bf16[8,1,32,128]{3,2,1,0:T(8,128)(2,1)S(1)}, u32[]{:S(2)}, u32[]{:S(2)}) %collective-permute-start.18) | collective-permute-done | bytes 65568 | tf_op jit(solution)/shard_map/ppermute | solution.py:29
  209.7 0.9 pad_maximum_fusion.5
  210.6 17.7 %all-reduce.16.cloned.1.call-done = f32[3,4,32,128]{3,0,2,1:T(4,128)} async-done(((f32[3,4,32,128]{3,0,2,1:T(4,128)}), f32[3,4,32,128]{3,0,2,1:T(4,128)}) %all-reduce.16.cloned.1.call-update) | async-done | bytes 196624 | tf_op jit(solution)/shard_map/psum | solution.py:139
  228.4 1.4 select_convert_fusion
  233.9 0.4 fusion.30
  237.9 3.7 %collective-permute-start.20 = (bf16[3,1,32,128]{3,0,2,1:T(4,128)(2,1)S(1)}, bf16[3,1,32,128]{3,0,2,1:T(4,128)(2,1)S(1)}, u32[]{:S(2)}, u32[]{:S(2)}) collective-permute-start(bf16[3,1,32,128]{3,0,2,1:T(4,128)(2,1)S(1)} %get-tuple-element.53), channel_id=1, source_target_pairs={{0,4},{4,8},{8,12},{1,5},{5,9},{9,13},{2,6},{6,10},{10,14},{3,7},{... | collective-permute-start | bytes 73736 | tf_op jit(solution)/shard_map/ppermute | solution.py:17
  241.5 1.3 collective-permute-start.21
  243.1 4.2 %collective-permute-done.21 = bf16[3,1,32,128]{3,0,2,1:T(4,128)(2,1)S(1)} collective-permute-done((bf16[3,1,32,128]{3,0,2,1:T(4,128)(2,1)S(1)}, bf16[3,1,32,128]{3,0,2,1:T(4,128)(2,1)S(1)}, u32[]{:S(2)}, u32[]{:S(2)}) %collective-permute-start.21) | collective-permute-done | bytes 24608 | tf_op jit(solution)/shard_map/ppermute | solution.py:19
  247.4 3.4 %collective-permute-start.22 = (bf16[3,6,1,128]{3,0,2,1:T(4,128)(2,1)S(1)}, bf16[3,6,1,128]{3,0,2,1:T(4,128)(2,1)S(1)}, u32[]{:S(2)}, u32[]{:S(2)}) collective-permute-start(bf16[3,6,1,128]{3,0,2,1:T(4,128)(2,1)S(1)} %get-tuple-element.45), channel_id=1, source_target_pairs={{0,2},{1,3},{4,6},{5,7},{8,10},{9,11},{12,14},{13,15},{16,18},{17,... | collective-permute-start | bytes 13832 | tf_op jit(solution)/shard_map/ppermute | solution.py:17
  250.7 1.3 collective-permute-start.23
  252.4 37.5 %psum.71 = f32[3,8,3,3,3]{1,4,3,2,0:T(4,128)} all-reduce(f32[3,8,3,3,3]{1,4,3,2,0:T(4,128)S(1)} %copy.170), channel_id=1, replica_groups=mesh['crops'=2,'xy'=4,'gz'=2,'lab'=2] {'xy','gz'}, use_global_device_ids=true, to_apply=%region_17.18 | all-reduce | flops 648 | bytes 5184 | tf_op jit(solution)/shard_map/psum | solution.py:167
  290.0 0.5 select_maximum_fusion
  293.8 0.4 copy-done.76
  295.1 0.4 copy-done.74
  297.8 0.4 copy-done.66
  301.0 0.4 copy-done.56
  302.4 0.4 copy-done.52
  304.4 0.7 copy.115
  (326 shorter events, 30.8 us)
Async XLA Ops:
  7.2 55.5 %all-reduce.14.cloned.1.call-start = ((), (), s32[]{:S(2)}) async-start(), calls=%async_computation | async-start | bytes 262144 | tf_op jit(solution)/shard_map/psum | solution.py:65
  8.4 14.6 %collective-permute-start.1 = (bf16[8,1,32,128]{3,0,2,1:T(8,128)(2,1)S(1)}, bf16[8,1,32,128]{3,0,2,1:T(8,128)(2,1)S(1)}, u32[]{:S(2)}, u32[]{:S(2)}) collective-permute-start(bf16[8,1,32,128]{3,0,2,1:T(8,128)(2,1)S(1)} %get-tuple-element.41), channel_id=1, source_target_pairs={{4,0},{8,4},{12,8},{5,1},{9,5},{13,9},{6,2},{10,6},{14,10},{7,3},{... | collective-permute-start | bytes 196616 | tf_op jit(solution)/shard_map/ppermute | solution.py:19
  9.7 13.1 %collective-permute-start = (bf16[8,1,32,128]{3,0,2,1:T(8,128)(2,1)S(1)}, bf16[8,1,32,128]{3,0,2,1:T(8,128)(2,1)S(1)}, u32[]{:S(2)}, u32[]{:S(2)}) collective-permute-start(bf16[8,1,32,128]{3,0,2,1:T(8,128)(2,1)S(1)} %get-tuple-element.42), channel_id=1, source_target_pairs={{0,4},{4,8},{8,12},{1,5},{5,9},{9,13},{2,6},{6,10},{10,14},{3,7},{... | collective-permute-start | bytes 196616 | tf_op jit(solution)/shard_map/ppermute | solution.py:17
  16.2 11.6 %collective-permute-start.4 = (bf16[4,1,32,128]{3,2,1,0:T(8,128)(2,1)S(1)}, bf16[4,1,32,128]{3,2,1,0:T(8,128)(2,1)S(1)}, u32[]{:S(2)}, u32[]{:S(2)}) collective-permute-start(bf16[4,1,32,128]{3,2,1,0:T(8,128)(2,1)S(1)} %get-tuple-element.59), channel_id=1, source_target_pairs={{0,4},{4,8},{8,12},{1,5},{5,9},{9,13},{2,6},{6,10},{10,14},{3,7},{... | collective-permute-start | bytes 98312 | tf_op jit(solution)/shard_map/ppermute | solution.py:17
  20.3 7.5 %collective-permute-start.5 = (bf16[4,1,32,128]{3,2,1,0:T(8,128)(2,1)S(1)}, bf16[4,1,32,128]{3,2,1,0:T(8,128)(2,1)S(1)}, u32[]{:S(2)}, u32[]{:S(2)}) collective-permute-start(bf16[4,1,32,128]{3,2,1,0:T(8,128)(2,1)S(1)} %get-tuple-element.60), channel_id=1, source_target_pairs={{4,0},{8,4},{12,8},{5,1},{9,5},{13,9},{6,2},{10,6},{14,10},{7,3},{... | collective-permute-start | bytes 98312 | tf_op jit(solution)/shard_map/ppermute | solution.py:19
  22.5 11.6 %copy-start.47 = (bf16[3,8,1,1,1]{1,4,3,2,0:T(2,128)(2,1)}, bf16[3,8,1,1,1]{1,4,3,2,0:T(2,128)(2,1)S(1)}, u32[]{:S(2)}) copy-start(bf16[3,8,1,1,1]{1,4,3,2,0:T(2,128)(2,1)S(1)} %get-tuple-element.64) | copy-start | bytes 148
  22.5 11.9 %copy-start.45 = (bf16[3,8,1,1,1]{1,4,3,2,0:T(2,128)(2,1)}, bf16[3,8,1,1,1]{1,4,3,2,0:T(2,128)(2,1)S(1)}, u32[]{:S(2)}) copy-start(bf16[3,8,1,1,1]{1,4,3,2,0:T(2,128)(2,1)S(1)} %get-tuple-element.67) | copy-start | bytes 148
  22.5 12.2 %copy-start.43 = (bf16[3,8,1,1,1]{1,4,3,2,0:T(2,128)(2,1)}, bf16[3,8,1,1,1]{1,4,3,2,0:T(2,128)(2,1)S(1)}, u32[]{:S(2)}) copy-start(bf16[3,8,1,1,1]{1,4,3,2,0:T(2,128)(2,1)S(1)} %get-tuple-element.70) | copy-start | bytes 148
  22.6 12.5 %copy-start.41 = (bf16[3,8,1,1,1]{1,4,3,2,0:T(2,128)(2,1)}, bf16[3,8,1,1,1]{1,4,3,2,0:T(2,128)(2,1)S(1)}, u32[]{:S(2)}) copy-start(bf16[3,8,1,1,1]{1,4,3,2,0:T(2,128)(2,1)S(1)} %get-tuple-element.76) | copy-start | bytes 148
  22.6 12.7 %copy-start.39 = (bf16[3,8,1,1,1]{1,4,3,2,0:T(2,128)(2,1)}, bf16[3,8,1,1,1]{1,4,3,2,0:T(2,128)(2,1)S(1)}, u32[]{:S(2)}) copy-start(bf16[3,8,1,1,1]{1,4,3,2,0:T(2,128)(2,1)S(1)} %get-tuple-element.79) | copy-start | bytes 148
  22.6 13.0 %copy-start.37 = (bf16[3,8,1,1,1]{1,4,3,2,0:T(2,128)(2,1)}, bf16[3,8,1,1,1]{1,4,3,2,0:T(2,128)(2,1)S(1)}, u32[]{:S(2)}) copy-start(bf16[3,8,1,1,1]{1,4,3,2,0:T(2,128)(2,1)S(1)} %get-tuple-element.82) | copy-start | bytes 148
  22.6 13.3 %copy-start.35 = (bf16[3,8,1,1,1]{1,4,3,2,0:T(2,128)(2,1)}, bf16[3,8,1,1,1]{1,4,3,2,0:T(2,128)(2,1)S(1)}, u32[]{:S(2)}) copy-start(bf16[3,8,1,1,1]{1,4,3,2,0:T(2,128)(2,1)S(1)} %get-tuple-element.88) | copy-start | bytes 148
  22.6 13.6 %copy-start.33 = (bf16[3,8,1,1,1]{1,4,3,2,0:T(2,128)(2,1)}, bf16[3,8,1,1,1]{1,4,3,2,0:T(2,128)(2,1)S(1)}, u32[]{:S(2)}) copy-start(bf16[3,8,1,1,1]{1,4,3,2,0:T(2,128)(2,1)S(1)} %get-tuple-element.86) | copy-start | bytes 148
  22.6 13.8 %copy-start.79 = (bf16[3,8,1,1,1]{1,4,3,2,0:T(2,128)(2,1)}, bf16[3,8,1,1,1]{1,4,3,2,0:T(2,128)(2,1)S(1)}, u32[]{:S(2)}) copy-start(bf16[3,8,1,1,1]{1,4,3,2,0:T(2,128)(2,1)S(1)} %get-tuple-element.87) | copy-start | bytes 148
  22.6 14.0 %copy-start.77 = (bf16[3,8,1,1,1]{1,4,3,2,0:T(2,128)(2,1)}, bf16[3,8,1,1,1]{1,4,3,2,0:T(2,128)(2,1)S(1)}, u32[]{:S(2)}) copy-start(bf16[3,8,1,1,1]{1,4,3,2,0:T(2,128)(2,1)S(1)} %get-tuple-element.85) | copy-start | bytes 148
  22.6 14.3 %copy-start.75 = (bf16[3,8,1,1,1]{1,4,3,2,0:T(2,128)(2,1)}, bf16[3,8,1,1,1]{1,4,3,2,0:T(2,128)(2,1)S(1)}, u32[]{:S(2)}) copy-start(bf16[3,8,1,1,1]{1,4,3,2,0:T(2,128)(2,1)S(1)} %get-tuple-element.84) | copy-start | bytes 148
  22.6 14.5 %copy-start.31 = (bf16[3,8,1,1,1]{1,4,3,2,0:T(2,128)(2,1)}, bf16[3,8,1,1,1]{1,4,3,2,0:T(2,128)(2,1)S(1)}, u32[]{:S(2)}) copy-start(bf16[3,8,1,1,1]{1,4,3,2,0:T(2,128)(2,1)S(1)} %get-tuple-element.83) | copy-start | bytes 148
  22.6 15.0 %copy-start.73 = (bf16[3,8,1,1,1]{1,4,3,2,0:T(2,128)(2,1)}, bf16[3,8,1,1,1]{1,4,3,2,0:T(2,128)(2,1)S(1)}, u32[]{:S(2)}) copy-start(bf16[3,8,1,1,1]{1,4,3,2,0:T(2,128)(2,1)S(1)} %get-tuple-element.81) | copy-start | bytes 148
  22.7 15.2 %copy-start.71 = (bf16[3,8,1,1,1]{1,4,3,2,0:T(2,128)(2,1)}, bf16[3,8,1,1,1]{1,4,3,2,0:T(2,128)(2,1)S(1)}, u32[]{:S(2)}) copy-start(bf16[3,8,1,1,1]{1,4,3,2,0:T(2,128)(2,1)S(1)} %get-tuple-element.80) | copy-start | bytes 148
  22.7 15.4 %copy-start.69 = (bf16[3,8,1,1,1]{1,4,3,2,0:T(2,128)(2,1)}, bf16[3,8,1,1,1]{1,4,3,2,0:T(2,128)(2,1)S(1)}, u32[]{:S(2)}) copy-start(bf16[3,8,1,1,1]{1,4,3,2,0:T(2,128)(2,1)S(1)} %get-tuple-element.78) | copy-start | bytes 148
  22.7 15.6 %copy-start.67 = (bf16[3,8,1,1,1]{1,4,3,2,0:T(2,128)(2,1)}, bf16[3,8,1,1,1]{1,4,3,2,0:T(2,128)(2,1)S(1)}, u32[]{:S(2)}) copy-start(bf16[3,8,1,1,1]{1,4,3,2,0:T(2,128)(2,1)S(1)} %get-tuple-element.77) | copy-start | bytes 148
  22.7 15.9 %copy-start.65 = (bf16[3,8,1,1,1]{1,4,3,2,0:T(2,128)(2,1)}, bf16[3,8,1,1,1]{1,4,3,2,0:T(2,128)(2,1)S(1)}, u32[]{:S(2)}) copy-start(bf16[3,8,1,1,1]{1,4,3,2,0:T(2,128)(2,1)S(1)} %get-tuple-element.75) | copy-start | bytes 148
  22.7 16.1 %copy-start.63 = (bf16[3,8,1,1,1]{1,4,3,2,0:T(2,128)(2,1)}, bf16[3,8,1,1,1]{1,4,3,2,0:T(2,128)(2,1)S(1)}, u32[]{:S(2)}) copy-start(bf16[3,8,1,1,1]{1,4,3,2,0:T(2,128)(2,1)S(1)} %get-tuple-element.74) | copy-start | bytes 148
  22.7 16.3 %copy-start.61 = (bf16[3,8,1,1,1]{1,4,3,2,0:T(2,128)(2,1)}, bf16[3,8,1,1,1]{1,4,3,2,0:T(2,128)(2,1)S(1)}, u32[]{:S(2)}) copy-start(bf16[3,8,1,1,1]{1,4,3,2,0:T(2,128)(2,1)S(1)} %get-tuple-element.73) | copy-start | bytes 148
  22.7 16.6 %copy-start.59 = (bf16[3,8,1,1,1]{1,4,3,2,0:T(2,128)(2,1)}, bf16[3,8,1,1,1]{1,4,3,2,0:T(2,128)(2,1)S(1)}, u32[]{:S(2)}) copy-start(bf16[3,8,1,1,1]{1,4,3,2,0:T(2,128)(2,1)S(1)} %get-tuple-element.72) | copy-start | bytes 148
  22.7 16.8 %copy-start.57 = (bf16[3,8,1,1,1]{1,4,3,2,0:T(2,128)(2,1)}, bf16[3,8,1,1,1]{1,4,3,2,0:T(2,128)(2,1)S(1)}, u32[]{:S(2)}) copy-start(bf16[3,8,1,1,1]{1,4,3,2,0:T(2,128)(2,1)S(1)} %get-tuple-element.71) | copy-start | bytes 148
  22.7 17.1 %copy-start.55 = (bf16[3,8,1,1,1]{1,4,3,2,0:T(2,128)(2,1)}, bf16[3,8,1,1,1]{1,4,3,2,0:T(2,128)(2,1)S(1)}, u32[]{:S(2)}) copy-start(bf16[3,8,1,1,1]{1,4,3,2,0:T(2,128)(2,1)S(1)} %get-tuple-element.69) | copy-start | bytes 148
  22.7 17.3 %copy-start.53 = (bf16[3,8,1,1,1]{1,4,3,2,0:T(2,128)(2,1)}, bf16[3,8,1,1,1]{1,4,3,2,0:T(2,128)(2,1)S(1)}, u32[]{:S(2)}) copy-start(bf16[3,8,1,1,1]{1,4,3,2,0:T(2,128)(2,1)S(1)} %get-tuple-element.68) | copy-start | bytes 148
  22.8 17.5 %copy-start.51 = (bf16[3,8,1,1,1]{1,4,3,2,0:T(2,128)(2,1)}, bf16[3,8,1,1,1]{1,4,3,2,0:T(2,128)(2,1)S(1)}, u32[]{:S(2)}) copy-start(bf16[3,8,1,1,1]{1,4,3,2,0:T(2,128)(2,1)S(1)} %get-tuple-element.66) | copy-start | bytes 148
  22.8 18.3 %copy-start.49 = (bf16[3,8,1,1,1]{1,4,3,2,0:T(2,128)(2,1)}, bf16[3,8,1,1,1]{1,4,3,2,0:T(2,128)(2,1)S(1)}, u32[]{:S(2)}) copy-start(bf16[3,8,1,1,1]{1,4,3,2,0:T(2,128)(2,1)S(1)} %get-tuple-element.63) | copy-start | bytes 148
  22.8 10.9 %copy-start.26 = (bf16[8,1,32,128]{3,0,2,1:T(8,128)(2,1)}, bf16[8,1,32,128]{3,0,2,1:T(8,128)(2,1)S(1)}, u32[]{:S(2)}) copy-start(bf16[8,1,32,128]{3,0,2,1:T(8,128)(2,1)S(1)} %collective-permute-done) | copy-start | bytes 196612
  23.0 10.7 %copy-start.23 = (bf16[8,1,32,128]{3,0,2,1:T(8,128)(2,1)}, bf16[8,1,32,128]{3,0,2,1:T(8,128)(2,1)S(1)}, u32[]{:S(2)}) copy-start(bf16[8,1,32,128]{3,0,2,1:T(8,128)(2,1)S(1)} %collective-permute-done.1) | copy-start | bytes 196612
  23.1 10.6 %collective-permute-start.2 = (bf16[8,6,1,128]{3,0,2,1:T(8,128)(2,1)S(1)}, bf16[8,6,1,128]{3,0,2,1:T(8,128)(2,1)S(1)}, u32[]{:S(2)}, u32[]{:S(2)}) collective-permute-start(bf16[8,6,1,128]{3,0,2,1:T(8,128)(2,1)S(1)} %get-tuple-element.30), channel_id=1, source_target_pairs={{0,2},{1,3},{4,6},{5,7},{8,10},{9,11},{12,14},{13,15},{16,18},{17,... | collective-permute-start | bytes 36872 | tf_op jit(solution)/shard_map/ppermute | solution.py:17
  26.5 7.2 %collective-permute-start.3 = (bf16[8,6,1,128]{3,0,2,1:T(8,128)(2,1)S(1)}, bf16[8,6,1,128]{3,0,2,1:T(8,128)(2,1)S(1)}, u32[]{:S(2)}, u32[]{:S(2)}) collective-permute-start(bf16[8,6,1,128]{3,0,2,1:T(8,128)(2,1)S(1)} %get-tuple-element.31), channel_id=1, source_target_pairs={{2,0},{3,1},{6,4},{7,5},{10,8},{11,9},{14,12},{15,13},{18,16},{19,... | collective-permute-start | bytes 36872 | tf_op jit(solution)/shard_map/ppermute | solution.py:19
  27.8 14.4 %collective-permute-start.6 = (bf16[4,6,1,128]{3,2,1,0:T(2,128)(2,1)S(1)}, bf16[4,6,1,128]{3,2,1,0:T(2,128)(2,1)S(1)}, u32[]{:S(2)}, u32[]{:S(2)}) collective-permute-start(bf16[4,6,1,128]{3,2,1,0:T(2,128)(2,1)S(1)} %get-tuple-element.51), channel_id=1, source_target_pairs={{0,2},{1,3},{4,6},{5,7},{8,10},{9,11},{12,14},{13,15},{16,18},{17,... | collective-permute-start | bytes 18440 | tf_op jit(solution)/shard_map/ppermute | solution.py:17
  32.4 9.8 %collective-permute-start.7 = (bf16[4,6,1,128]{3,2,1,0:T(2,128)(2,1)S(1)}, bf16[4,6,1,128]{3,2,1,0:T(2,128)(2,1)S(1)}, u32[]{:S(2)}, u32[]{:S(2)}) collective-permute-start(bf16[4,6,1,128]{3,2,1,0:T(2,128)(2,1)S(1)} %get-tuple-element.52), channel_id=1, source_target_pairs={{2,0},{3,1},{6,4},{7,5},{10,8},{11,9},{14,12},{15,13},{18,16},{19,... | collective-permute-start | bytes 18440 | tf_op jit(solution)/shard_map/ppermute | solution.py:19
  42.2 186.2 %all-reduce.16.cloned.1.call-start = ((), (), s32[]{:S(2)}) async-start(), calls=%async_computation.1 | async-start | bytes 524288 | tf_op jit(solution)/shard_map/psum | solution.py:139
  64.4 7.6 %collective-permute-start.9 = (f32[4,1,128]{2,0,1:T(4,128)S(1)}, f32[4,1,128]{2,0,1:T(4,128)S(1)}, u32[]{:S(2)}, u32[]{:S(2)}) collective-permute-start(f32[4,1,128]{2,0,1:T(4,128)S(1)} %bitcast.468), channel_id=1, source_target_pairs={{0,2},{1,3},{4,6},{5,7},{8,10},{9,11},{12,14},{13,15},{16,18},{17,... | collective-permute-start | bytes 6152 | tf_op jit(solution)/shard_map/ppermute | solution.py:29
  68.4 4.8 %collective-permute-start.8 = (f32[1,32,128]{2,1,0:T(8,128)S(1)}, f32[1,32,128]{2,1,0:T(8,128)S(1)}, u32[]{:S(2)}, u32[]{:S(2)}) collective-permute-start(f32[1,32,128]{2,1,0:T(8,128)S(1)} %bitcast.466), channel_id=1, source_target_pairs={{0,4},{4,8},{8,12},{1,5},{5,9},{9,13},{2,6},{6,10},{10,14},{3,7},{... | collective-permute-start | bytes 49160 | tf_op jit(solution)/shard_map/ppermute | solution.py:29
  93.9 18.1 %copy-start.83 = (f32[4]{0:T(128)}, f32[4]{0:T(128)S(1)}, u32[]{:S(2)}) copy-start(f32[4]{0:T(128)S(1)} %div.24) | copy-start | bytes 52
  112.0 2.9 collective-permute-start.10
  113.3 5.8 %collective-permute-start.11 = (bf16[4,1,32,128]{3,2,1,0:T(8,128)(2,1)S(1)}, bf16[4,1,32,128]{3,2,1,0:T(8,128)(2,1)S(1)}, u32[]{:S(2)}, u32[]{:S(2)}) collective-permute-start(bf16[4,1,32,128]{3,2,1,0:T(8,128)(2,1)S(1)} %get-tuple-element.58), channel_id=1, source_target_pairs={{4,0},{8,4},{12,8},{5,1},{9,5},{13,9},{6,2},{10,6},{14,10},{7,3},{... | collective-permute-start | bytes 98312 | tf_op jit(solution)/shard_map/ppermute | solution.py:19
  119.1 5.3 %collective-permute-start.12 = (bf16[4,6,1,128]{3,2,1,0:T(2,128)(2,1)S(1)}, bf16[4,6,1,128]{3,2,1,0:T(2,128)(2,1)S(1)}, u32[]{:S(2)}, u32[]{:S(2)}) collective-permute-start(bf16[4,6,1,128]{3,2,1,0:T(2,128)(2,1)S(1)} %get-tuple-element.49), channel_id=1, source_target_pairs={{0,2},{1,3},{4,6},{5,7},{8,10},{9,11},{12,14},{13,15},{16,18},{17,... | collective-permute-start | bytes 18440 | tf_op jit(solution)/shard_map/ppermute | solution.py:17
  122.9 5.6 %collective-permute-start.13 = (bf16[4,6,1,128]{3,2,1,0:T(2,128)(2,1)S(1)}, bf16[4,6,1,128]{3,2,1,0:T(2,128)(2,1)S(1)}, u32[]{:S(2)}, u32[]{:S(2)}) collective-permute-start(bf16[4,6,1,128]{3,2,1,0:T(2,128)(2,1)S(1)} %get-tuple-element.50), channel_id=1, source_target_pairs={{2,0},{3,1},{6,4},{7,5},{10,8},{11,9},{14,12},{15,13},{18,16},{19,... | collective-permute-start | bytes 18440 | tf_op jit(solution)/shard_map/ppermute | solution.py:19
  147.5 19.3 %copy-start.81 = (f32[4]{0:T(128)}, f32[4]{0:T(128)S(1)}, u32[]{:S(2)}) copy-start(f32[4]{0:T(128)S(1)} %div.26) | copy-start | bytes 52
  168.8 2.9 collective-permute-start.14
  170.1 5.8 %collective-permute-start.15 = (bf16[4,1,32,128]{3,2,1,0:T(8,128)(2,1)S(1)}, bf16[4,1,32,128]{3,2,1,0:T(8,128)(2,1)S(1)}, u32[]{:S(2)}, u32[]{:S(2)}) collective-permute-start(bf16[4,1,32,128]{3,2,1,0:T(8,128)(2,1)S(1)} %get-tuple-element.56), channel_id=1, source_target_pairs={{4,0},{8,4},{12,8},{5,1},{9,5},{13,9},{6,2},{10,6},{14,10},{7,3},{... | collective-permute-start | bytes 98312 | tf_op jit(solution)/shard_map/ppermute | solution.py:19
  176.0 3.5 %collective-permute-start.16 = (bf16[4,6,1,128]{3,2,1,0:T(2,128)(2,1)S(1)}, bf16[4,6,1,128]{3,2,1,0:T(2,128)(2,1)S(1)}, u32[]{:S(2)}, u32[]{:S(2)}) collective-permute-start(bf16[4,6,1,128]{3,2,1,0:T(2,128)(2,1)S(1)} %get-tuple-element.47), channel_id=1, source_target_pairs={{0,2},{1,3},{4,6},{5,7},{8,10},{9,11},{12,14},{13,15},{16,18},{17,... | collective-permute-start | bytes 18440 | tf_op jit(solution)/shard_map/ppermute | solution.py:17
  177.9 5.6 %collective-permute-start.17 = (bf16[4,6,1,128]{3,2,1,0:T(2,128)(2,1)S(1)}, bf16[4,6,1,128]{3,2,1,0:T(2,128)(2,1)S(1)}, u32[]{:S(2)}, u32[]{:S(2)}) collective-permute-start(bf16[4,6,1,128]{3,2,1,0:T(2,128)(2,1)S(1)} %get-tuple-element.48), channel_id=1, source_target_pairs={{2,0},{3,1},{6,4},{7,5},{10,8},{11,9},{14,12},{15,13},{18,16},{19,... | collective-permute-start | bytes 18440 | tf_op jit(solution)/shard_map/ppermute | solution.py:19
  183.7 17.6 %copy-start.87 = (f32[4]{0:T(128)S(1)}, f32[4]{0:T(128)}, u32[]{:S(2)}) copy-start(f32[4]{0:T(128)} %copy-done.86) | copy-start | bytes 52
  183.7 17.6 %copy-start.82 = (f32[4]{0:T(128)S(1)}, f32[4]{0:T(128)}, u32[]{:S(2)}) copy-start(f32[4]{0:T(128)} %copy-done.81) | copy-start | bytes 52
  183.7 17.6 %copy-start.84 = (f32[4]{0:T(128)S(1)}, f32[4]{0:T(128)}, u32[]{:S(2)}) copy-start(f32[4]{0:T(128)} %copy-done.83) | copy-start | bytes 52
  201.7 7.5 %collective-permute-start.19 = (f32[8,4,1,128]{3,2,1,0:T(1,128)S(1)}, f32[8,4,1,128]{3,2,1,0:T(1,128)S(1)}, u32[]{:S(2)}, u32[]{:S(2)}) collective-permute-start(f32[8,4,1,128]{3,2,1,0:T(1,128)S(1)} %fusion.176), channel_id=1, source_target_pairs={{2,0},{3,1},{6,4},{7,5},{10,8},{11,9},{14,12},{15,13},{18,16},{19,... | collective-permute-start | bytes 49160 | tf_op jit(solution)/shard_map/ppermute | solution.py:29
  203.0 6.2 %collective-permute-start.18 = (bf16[8,1,32,128]{3,2,1,0:T(8,128)(2,1)S(1)}, bf16[8,1,32,128]{3,2,1,0:T(8,128)(2,1)S(1)}, u32[]{:S(2)}, u32[]{:S(2)}) collective-permute-start(bf16[8,1,32,128]{3,2,1,0:T(8,128)(2,1)S(1)} %fusion.141), channel_id=1, source_target_pairs={{4,0},{8,4},{12,8},{5,1},{9,5},{13,9},{6,2},{10,6},{14,10},{7,3},{... | collective-permute-start | bytes 196616 | tf_op jit(solution)/shard_map/ppermute | solution.py:29
  209.6 18.8 %copy-start.15 = (pred[1,4,32,128]{3,0,2,1:T(4,128)(4,1)S(1)}, pred[1,4,32,128]{3,0,2,1:T(4,128)(4,1)}, u32[]{:S(2)}) copy-start(pred[1,4,32,128]{3,0,2,1:T(4,128)(4,1)} %copy-done.14) | copy-start | bytes 49156
  209.6 18.8 %copy-start.17 = (pred[1,4,32,128]{3,0,2,1:T(4,128)(4,1)S(1)}, pred[1,4,32,128]{3,0,2,1:T(4,128)(4,1)}, u32[]{:S(2)}) copy-start(pred[1,4,32,128]{3,0,2,1:T(4,128)(4,1)} %copy-done.16) | copy-start | bytes 49156
  209.6 18.8 %copy-start.19 = (pred[1,4,32,128]{3,0,2,1:T(4,128)(4,1)S(1)}, pred[1,4,32,128]{3,0,2,1:T(4,128)(4,1)}, u32[]{:S(2)}) copy-start(pred[1,4,32,128]{3,0,2,1:T(4,128)(4,1)} %copy-done.18) | copy-start | bytes 49156
  209.6 18.8 %copy-start.20 = (bf16[3,4,32,128]{3,0,2,1:T(4,128)(2,1)S(1)}, bf16[3,4,32,128]{3,0,2,1:T(4,128)(2,1)}, u32[]{:S(2)}) copy-start(bf16[3,4,32,128]{3,0,2,1:T(4,128)(2,1)} %all-reduce.14.cloned.1.call-done) | copy-start | bytes 294916
  237.9 5.3 %collective-permute-start.20 = (bf16[3,1,32,128]{3,0,2,1:T(4,128)(2,1)S(1)}, bf16[3,1,32,128]{3,0,2,1:T(4,128)(2,1)S(1)}, u32[]{:S(2)}, u32[]{:S(2)}) collective-permute-start(bf16[3,1,32,128]{3,0,2,1:T(4,128)(2,1)S(1)} %get-tuple-element.53), channel_id=1, source_target_pairs={{0,4},{4,8},{8,12},{1,5},{5,9},{9,13},{2,6},{6,10},{10,14},{3,7},{... | collective-permute-start | bytes 73736 | tf_op jit(solution)/shard_map/ppermute | solution.py:17
  241.5 5.8 %collective-permute-start.21 = (bf16[3,1,32,128]{3,0,2,1:T(4,128)(2,1)S(1)}, bf16[3,1,32,128]{3,0,2,1:T(4,128)(2,1)S(1)}, u32[]{:S(2)}, u32[]{:S(2)}) collective-permute-start(bf16[3,1,32,128]{3,0,2,1:T(4,128)(2,1)S(1)} %get-tuple-element.54), channel_id=1, source_target_pairs={{4,0},{8,4},{12,8},{5,1},{9,5},{13,9},{6,2},{10,6},{14,10},{7,3},{... | collective-permute-start | bytes 73736 | tf_op jit(solution)/shard_map/ppermute | solution.py:19
  243.1 47.3 %copy-start.48 = (bf16[3,8,1,1,1]{1,4,3,2,0:T(2,128)(2,1)S(1)}, bf16[3,8,1,1,1]{1,4,3,2,0:T(2,128)(2,1)}, u32[]{:S(2)}) copy-start(bf16[3,8,1,1,1]{1,4,3,2,0:T(2,128)(2,1)} %copy-done.47) | copy-start | bytes 148
  247.4 42.6 %collective-permute-start.22 = (bf16[3,6,1,128]{3,0,2,1:T(4,128)(2,1)S(1)}, bf16[3,6,1,128]{3,0,2,1:T(4,128)(2,1)S(1)}, u32[]{:S(2)}, u32[]{:S(2)}) collective-permute-start(bf16[3,6,1,128]{3,0,2,1:T(4,128)(2,1)S(1)} %get-tuple-element.45), channel_id=1, source_target_pairs={{0,2},{1,3},{4,6},{5,7},{8,10},{9,11},{12,14},{13,15},{16,18},{17,... | collective-permute-start | bytes 13832 | tf_op jit(solution)/shard_map/ppermute | solution.py:17
  250.7 39.2 %collective-permute-start.23 = (bf16[3,6,1,128]{3,0,2,1:T(4,128)(2,1)S(1)}, bf16[3,6,1,128]{3,0,2,1:T(4,128)(2,1)S(1)}, u32[]{:S(2)}, u32[]{:S(2)}) collective-permute-start(bf16[3,6,1,128]{3,0,2,1:T(4,128)(2,1)S(1)} %get-tuple-element.46), channel_id=1, source_target_pairs={{2,0},{3,1},{6,4},{7,5},{10,8},{11,9},{14,12},{15,13},{18,16},{19,... | collective-permute-start | bytes 13832 | tf_op jit(solution)/shard_map/ppermute | solution.py:19
  252.4 38.4 %copy-start.46 = (bf16[3,8,1,1,1]{1,4,3,2,0:T(2,128)(2,1)S(1)}, bf16[3,8,1,1,1]{1,4,3,2,0:T(2,128)(2,1)}, u32[]{:S(2)}) copy-start(bf16[3,8,1,1,1]{1,4,3,2,0:T(2,128)(2,1)} %copy-done.45) | copy-start | bytes 148
  (50 other events, 153.8 us)
Sparse Core Ops, SparseCore 0:
  42.3 20.3 all-reduce.13
  210.8 17.5 all-reduce.15
where the time goes:
time: 313 us; the launch traced here: 312 us
  blocking collectives  128 us (41%)
  waiting for transfers between devices  65.5 us (21%)
  starting transfers between devices  55.7 us (18%)
  matrix products  23.8 us (8%)
  between operations  15.9 us (5%)
  local copies, waits for them, and re-layouts  11.5 us (4%)
  other arithmetic  11.3 us (4%)
    psum x3, blocking collectives, squares(): lax.psum(jnp.sum(remainder_grid * remainder_grid, axis=(1, 2, 3)), ('xy',...  56.4 us
    psum x1, blocking collectives, local(): grad_filter = lax.psum(filter_part, ('xy', 'gz'))  37.5 us
    psum x2, blocking collectives, local(): lax.psum(jnp.sum(direction * picture_pixels_flat, axis=(1, 2, 3)), ('xy',...  34.5 us
    ppermute x10, starting transfers between devices, with_halo(): lax.ppermute(tail, axis, [(i, (i + 1) % count) for i in range(ends)])  32.9 us
    ppermute x10, waiting for transfers between devices, with_halo(): lax.ppermute(head, axis, [((i + 1) % count, i) for i in range(ends)])  20.9 us
    psum x1, waiting for transfers between devices, local(): lax.psum(correlate(own_filt, own_wide, rows_x, rows_z, rows_y).astype(jnp...  20.3 us
    psum x1, waiting for transfers between devices, local(): edge_grad = lax.psum(jnp.stack(partial_grads), 'lab')  17.7 us
    ppermute x10, starting transfers between devices, with_halo(): lax.ppermute(head, axis, [((i + 1) % count, i) for i in range(ends)])  12.9 us
  transfers between devices with their start and end apart: 26, of which 11 were waited for; matrix products, arithmetic and copies ran while one was open for 4% of the time, Pallas kernels for 0%

commit v1 on v0

--- a/solution.py
+++ b/solution.py
@@ -49,7 +49,7 @@
 
 
 def squares(remainder_grid):
-    return lax.psum(jnp.sum(remainder_grid * remainder_grid, axis=(1, 2, 3)), ("xy", "gz"))[
+    return lax.psum(lax.psum(jnp.sum(remainder_grid * remainder_grid, axis=(1, 2, 3)), "gz"), "xy")[
         :, None, None, None
     ]
 

time: 313 us -> 323 us (1.032)
  blocking collectives: 128 us -> 135 us
    psum x2 -> x3, blocking collectives: 34.5 us -> 55 us  [local(): lax.psum(jnp.sum(direction * picture_pixels_flat, axis=(1, 2, 3)), ('xy',...]
    psum x3 -> x6, blocking collectives: 56.4 us -> 42.4 us  [the longest x3 27.6 us: squares(): lax.psum(lax.psum(jnp.sum(remainder_grid * remainder_grid, axis=(1, 2, 3)...]
  transfers between devices with their start and end apart: 26 -> 26, of which waited for: 11 -> 11; matrix products, arithmetic and copies ran while one was open for 4% -> 3% of each run, Pallas kernels for 0% -> 0%
where the time goes in v1:
time: 323 us; the launch traced here: 322 us
  blocking collectives  135 us (42%)
  waiting for transfers between devices  65.6 us (20%)
  starting transfers between devices  58.9 us (18%)
  matrix products  23.8 us (7%)
  between operations  15.9 us (5%)
  local copies, waits for them, and re-layouts  11.5 us (4%)
  other arithmetic  11.3 us (3%)
    psum x3, blocking collectives, local(): lax.psum(jnp.sum(direction * picture_pixels_flat, axis=(1, 2, 3)), ('xy',...  55 us
    psum x1, blocking collectives, local(): grad_filter = lax.psum(filter_part, ('xy', 'gz'))  37.5 us
    ppermute x10, starting transfers between devices, with_halo(): lax.ppermute(tail, axis, [(i, (i + 1) % count) for i in range(ends)])  36.1 us
    psum x3, blocking collectives, squares(): lax.psum(lax.psum(jnp.sum(remainder_grid * remainder_grid, axis=(1, 2, 3)...  27.6 us
    ppermute x10, waiting for transfers between devices, with_halo(): lax.ppermute(head, axis, [((i + 1) % count, i) for i in range(ends)])  20.9 us
    psum x1, waiting for transfers between devices, local(): lax.psum(correlate(own_filt, own_wide, rows_x, rows_z, rows_y).astype(jnp...  20.3 us
    psum x1, waiting for transfers between devices, local(): edge_grad = lax.psum(jnp.stack(partial_grads), 'lab')  17.7 us
    psum x3, blocking collectives, squares(): lax.psum(jnp.sum(remainder_grid * remainder_grid, axis=(1, 2, 3)), 'gz')  14.8 us
  transfers between devices with their start and end apart: 26, of which 11 were waited for; matrix products, arithmetic and copies ran while one was open for 3% of the time, Pallas kernels for 0%

profile of v1, /device:TPU:0, one launch (start us, length us, event | category | flops | bytes accessed | tf_op | source)
XLA Modules:
  0.0 321.9 jit_solution(2962563963353542698)
XLA Ops:
  7.2 1.2 copy.105
  8.4 1.3 collective-permute-start.1
  9.7 5.6 %collective-permute-start = (bf16[8,1,32,128]{3,0,2,1:T(8,128)(2,1)S(1)}, bf16[8,1,32,128]{3,0,2,1:T(8,128)(2,1)S(1)}, u32[]{:S(2)}, u32[]{:S(2)}) collective-permute-start(bf16[8,1,32,128]{3,0,2,1:T(8,128)(2,1)S(1)} %get-tuple-element.40), channel_id=1, source_target_pairs={{0,4},{4,8},{8,12},{1,5},{5,9},{9,13},{2,6},{6,10},{10,14},{3,7},{... | collective-permute-start | bytes 196616 | tf_op jit(solution)/shard_map/ppermute | solution.py:17
  15.3 0.8 compare_convert_fusion
  16.2 4.1 %collective-permute-start.4 = (bf16[4,1,32,128]{3,2,1,0:T(8,128)(2,1)S(1)}, bf16[4,1,32,128]{3,2,1,0:T(8,128)(2,1)S(1)}, u32[]{:S(2)}, u32[]{:S(2)}) collective-permute-start(bf16[4,1,32,128]{3,2,1,0:T(8,128)(2,1)S(1)} %get-tuple-element.57), channel_id=1, source_target_pairs={{0,4},{4,8},{8,12},{1,5},{5,9},{9,13},{2,6},{6,10},{10,14},{3,7},{... | collective-permute-start | bytes 98312 | tf_op jit(solution)/shard_map/ppermute | solution.py:17
  20.3 1.3 collective-permute-start.5
  21.6 0.8 fusion.315
  23.1 3.4 %collective-permute-start.2 = (bf16[8,6,1,128]{3,0,2,1:T(8,128)(2,1)S(1)}, bf16[8,6,1,128]{3,0,2,1:T(8,128)(2,1)S(1)}, u32[]{:S(2)}, u32[]{:S(2)}) collective-permute-start(bf16[8,6,1,128]{3,0,2,1:T(8,128)(2,1)S(1)} %get-tuple-element.28), channel_id=1, source_target_pairs={{0,2},{1,3},{4,6},{5,7},{8,10},{9,11},{12,14},{13,15},{16,18},{17,... | collective-permute-start | bytes 36872 | tf_op jit(solution)/shard_map/ppermute | solution.py:17
  26.5 1.3 collective-permute-start.3
  27.8 4.5 %collective-permute-start.6 = (bf16[4,6,1,128]{3,2,1,0:T(2,128)(2,1)S(1)}, bf16[4,6,1,128]{3,2,1,0:T(2,128)(2,1)S(1)}, u32[]{:S(2)}, u32[]{:S(2)}) collective-permute-start(bf16[4,6,1,128]{3,2,1,0:T(2,128)(2,1)S(1)} %get-tuple-element.49), channel_id=1, source_target_pairs={{0,2},{1,3},{4,6},{5,7},{8,10},{9,11},{12,14},{13,15},{16,18},{17,... | collective-permute-start | bytes 18440 | tf_op jit(solution)/shard_map/ppermute | solution.py:17
  32.4 1.3 collective-permute-start.7
  33.7 0.4 fusion.48
  40.5 0.4 copy-done.24
  41.3 0.9 fusion.16
  42.4 20.3 %all-reduce.13.cloned.1.call-done = bf16[3,4,32,128]{3,0,2,1:T(4,128)(2,1)} async-done(((bf16[3,4,32,128]{3,0,2,1:T(4,128)(2,1)}), bf16[3,4,32,128]{3,0,2,1:T(4,128)(2,1)}) %all-reduce.13.cloned.1.call-update) | async-done | bytes 98320 | tf_op jit(solution)/shard_map/psum | solution.py:65
  63.0 1.3 add_select_fusion
  64.4 3.6 %collective-permute-start.9 = (f32[4,1,128]{2,0,1:T(4,128)S(1)}, f32[4,1,128]{2,0,1:T(4,128)S(1)}, u32[]{:S(2)}, u32[]{:S(2)}) collective-permute-start(f32[4,1,128]{2,0,1:T(4,128)S(1)} %bitcast.468), channel_id=1, source_target_pairs={{0,2},{1,3},{4,6},{5,7},{8,10},{9,11},{12,14},{13,15},{16,18},{17,... | collective-permute-start | bytes 6152 | tf_op jit(solution)/shard_map/ppermute | solution.py:29
  68.4 3.4 %collective-permute-start.8 = (f32[1,32,128]{2,1,0:T(8,128)S(1)}, f32[1,32,128]{2,1,0:T(8,128)S(1)}, u32[]{:S(2)}, u32[]{:S(2)}) collective-permute-start(f32[1,32,128]{2,1,0:T(8,128)S(1)} %bitcast.466), channel_id=1, source_target_pairs={{0,4},{4,8},{8,12},{1,5},{5,9},{9,13},{2,6},{6,10},{10,14},{3,7},{... | collective-permute-start | bytes 49160 | tf_op jit(solution)/shard_map/ppermute | solution.py:29
  71.9 1.3 collective-permute-done.8
  73.3 0.4 multiply_reduce_fusion.3
  73.8 4.9 %psum.84 = f32[4]{0:T(128)S(1)} all-reduce(f32[4]{0:T(128)S(1)} %get-tuple-element.13), channel_id=1, replica_groups=mesh['crops'=2,'xy'=4,'gz'=2,'lab'=2] {'gz'}, use_global_device_ids=true, to_apply=%region_1.2 | all-reduce | flops 4 | bytes 32 | tf_op jit(solution)/shard_map/psum | solution.py:52
  78.8 20.7 %psum.87 = f32[4]{0:T(128)S(1)} all-reduce(f32[4]{0:T(128)S(1)} %get-tuple-element.12), channel_id=1, replica_groups=mesh['crops'=2,'xy'=4,'gz'=2,'lab'=2] {'xy','gz'}, use_global_device_ids=true, to_apply=%region_5.6 | all-reduce | flops 4 | bytes 32 | tf_op jit(solution)/shard_map/psum | solution.py:120
  99.4 8.4 %psum.85 = f32[4]{0:T(128)S(1)} all-reduce(f32[4]{0:T(128)S(1)} %psum.84), channel_id=1, replica_groups=mesh['crops'=2,'xy'=4,'gz'=2,'lab'=2] {'xy'}, use_global_device_ids=true, to_apply=%region_2.3 | all-reduce | flops 4 | bytes 32 | tf_op jit(solution)/shard_map/psum | solution.py:52
  108.0 4.9 %psum.88 = f32[4]{0:T(128)S(1)} all-reduce(f32[4]{0:T(128)S(1)} %get-tuple-element.20), channel_id=1, replica_groups=mesh['crops'=2,'xy'=4,'gz'=2,'lab'=2] {'gz'}, use_global_device_ids=true, to_apply=%region_7.8 | all-reduce | flops 4 | bytes 32 | tf_op jit(solution)/shard_map/psum | solution.py:52
  112.9 10.3 %psum.89 = f32[4]{0:T(128)S(1)} all-reduce(f32[4]{0:T(128)S(1)} %psum.88), channel_id=1, replica_groups=mesh['crops'=2,'xy'=4,'gz'=2,'lab'=2] {'xy'}, use_global_device_ids=true, to_apply=%region_8.9 | all-reduce | flops 4 | bytes 32 | tf_op jit(solution)/shard_map/psum | solution.py:52
  123.3 0.5 copy-done.85
  123.9 1.9 collective-permute-start.10
  125.8 1.3 collective-permute-start.11
  127.4 4.2 %collective-permute-done.11 = bf16[4,1,32,128]{3,2,1,0:T(8,128)(2,1)S(1)} collective-permute-done((bf16[4,1,32,128]{3,2,1,0:T(8,128)(2,1)S(1)}, bf16[4,1,32,128]{3,2,1,0:T(8,128)(2,1)S(1)}, u32[]{:S(2)}, u32[]{:S(2)}) %collective-permute-start.11) | collective-permute-done | bytes 32800 | tf_op jit(solution)/shard_map/ppermute | solution.py:19
  131.7 2.4 collective-permute-start.12
  134.0 1.3 collective-permute-start.13
  135.5 4.1 %collective-permute-done.13 = bf16[4,6,1,128]{3,2,1,0:T(2,128)(2,1)S(1)} collective-permute-done((bf16[4,6,1,128]{3,2,1,0:T(2,128)(2,1)S(1)}, bf16[4,6,1,128]{3,2,1,0:T(2,128)(2,1)S(1)}, u32[]{:S(2)}, u32[]{:S(2)}) %collective-permute-start.13) | collective-permute-done | bytes 6176 | tf_op jit(solution)/shard_map/ppermute | solution.py:19
  139.8 0.9 multiply_reduce_fusion.1
  140.7 17.2 %psum.90 = f32[4]{0:T(128)S(1)} all-reduce(f32[4]{0:T(128)} %get-tuple-element.16), channel_id=1, replica_groups=mesh['crops'=2,'xy'=4,'gz'=2,'lab'=2] {'xy','gz'}, use_global_device_ids=true, to_apply=%region_10.11 | all-reduce | flops 4 | bytes 32 | tf_op jit(solution)/shard_map/psum | solution.py:120
  157.9 0.7 div.26
  158.8 4.9 %psum.91 = f32[4]{0:T(128)S(1)} all-reduce(f32[4]{0:T(128)S(1)} %multiply_reduce_fusion), channel_id=1, replica_groups=mesh['crops'=2,'xy'=4,'gz'=2,'lab'=2] {'gz'}, use_global_device_ids=true, to_apply=%region_12.13 | all-reduce | flops 4 | bytes 32 | tf_op jit(solution)/shard_map/psum | solution.py:52
  163.7 8.9 %psum.92 = f32[4]{0:T(128)S(1)} all-reduce(f32[4]{0:T(128)S(1)} %psum.91), channel_id=1, replica_groups=mesh['crops'=2,'xy'=4,'gz'=2,'lab'=2] {'xy'}, use_global_device_ids=true, to_apply=%region_13.14 | all-reduce | flops 4 | bytes 32 | tf_op jit(solution)/shard_map/psum | solution.py:52
  172.6 0.6 copy-done.86
  173.2 0.7 div.27
  173.8 0.8 fusion.306
  174.6 3.3 %collective-permute-start.14 = (bf16[4,1,32,128]{3,2,1,0:T(8,128)(2,1)S(1)}, bf16[4,1,32,128]{3,2,1,0:T(8,128)(2,1)S(1)}, u32[]{:S(2)}, u32[]{:S(2)}) collective-permute-start(bf16[4,1,32,128]{3,2,1,0:T(8,128)(2,1)S(1)} %get-tuple-element.53), channel_id=1, source_target_pairs={{0,4},{4,8},{8,12},{1,5},{5,9},{9,13},{2,6},{6,10},{10,14},{3,7},{... | collective-permute-start | bytes 98312 | tf_op jit(solution)/shard_map/ppermute | solution.py:17
  178.0 1.3 collective-permute-start.15
  179.5 4.2 %collective-permute-done.15 = bf16[4,1,32,128]{3,2,1,0:T(8,128)(2,1)S(1)} collective-permute-done((bf16[4,1,32,128]{3,2,1,0:T(8,128)(2,1)S(1)}, bf16[4,1,32,128]{3,2,1,0:T(8,128)(2,1)S(1)}, u32[]{:S(2)}, u32[]{:S(2)}) %collective-permute-start.15) | collective-permute-done | bytes 32800 | tf_op jit(solution)/shard_map/ppermute | solution.py:19
  183.8 3.9 %collective-permute-start.16 = (bf16[4,6,1,128]{3,2,1,0:T(2,128)(2,1)S(1)}, bf16[4,6,1,128]{3,2,1,0:T(2,128)(2,1)S(1)}, u32[]{:S(2)}, u32[]{:S(2)}) collective-permute-start(bf16[4,6,1,128]{3,2,1,0:T(2,128)(2,1)S(1)} %get-tuple-element.45), channel_id=1, source_target_pairs={{0,2},{1,3},{4,6},{5,7},{8,10},{9,11},{12,14},{13,15},{16,18},{17,... | collective-permute-start | bytes 18440 | tf_op jit(solution)/shard_map/ppermute | solution.py:17
  187.7 1.3 collective-permute-start.17
  189.2 4.1 %collective-permute-done.17 = bf16[4,6,1,128]{3,2,1,0:T(2,128)(2,1)S(1)} collective-permute-done((bf16[4,6,1,128]{3,2,1,0:T(2,128)(2,1)S(1)}, bf16[4,6,1,128]{3,2,1,0:T(2,128)(2,1)S(1)}, u32[]{:S(2)}, u32[]{:S(2)}) %collective-permute-start.17) | collective-permute-done | bytes 6176 | tf_op jit(solution)/shard_map/ppermute | solution.py:19
  193.5 0.4 fusion.71
  193.9 17.1 %psum.93 = f32[4]{0:T(128)S(1)} all-reduce(f32[4]{0:T(128)S(1)} %fusion.71), channel_id=1, replica_groups=mesh['crops'=2,'xy'=4,'gz'=2,'lab'=2] {'xy','gz'}, use_global_device_ids=true, to_apply=%region_15.16 | all-reduce | flops 4 | bytes 32 | tf_op jit(solution)/shard_map/psum | solution.py:120
  211.5 1.5 collective-permute-start.19
  212.9 1.3 collective-permute-start.18
  214.3 4.8 %collective-permute-done.18 = bf16[8,1,32,128]{3,2,1,0:T(8,128)(2,1)S(1)} collective-permute-done((bf16[8,1,32,128]{3,2,1,0:T(8,128)(2,1)S(1)}, bf16[8,1,32,128]{3,2,1,0:T(8,128)(2,1)S(1)}, u32[]{:S(2)}, u32[]{:S(2)}) %collective-permute-start.18) | collective-permute-done | bytes 65568 | tf_op jit(solution)/shard_map/ppermute | solution.py:29
  219.6 0.9 pad_maximum_fusion.5
  220.5 17.7 %all-reduce.15.cloned.1.call-done = f32[3,4,32,128]{3,0,2,1:T(4,128)} async-done(((f32[3,4,32,128]{3,0,2,1:T(4,128)}), f32[3,4,32,128]{3,0,2,1:T(4,128)}) %all-reduce.15.cloned.1.call-update) | async-done | bytes 196624 | tf_op jit(solution)/shard_map/psum | solution.py:139
  238.3 1.4 select_convert_fusion
  247.8 3.7 %collective-permute-start.20 = (bf16[3,1,32,128]{3,0,2,1:T(4,128)(2,1)S(1)}, bf16[3,1,32,128]{3,0,2,1:T(4,128)(2,1)S(1)}, u32[]{:S(2)}, u32[]{:S(2)}) collective-permute-start(bf16[3,1,32,128]{3,0,2,1:T(4,128)(2,1)S(1)} %get-tuple-element.51), channel_id=1, source_target_pairs={{0,4},{4,8},{8,12},{1,5},{5,9},{9,13},{2,6},{6,10},{10,14},{3,7},{... | collective-permute-start | bytes 73736 | tf_op jit(solution)/shard_map/ppermute | solution.py:17
  251.4 1.3 collective-permute-start.21
  253.0 4.2 %collective-permute-done.21 = bf16[3,1,32,128]{3,0,2,1:T(4,128)(2,1)S(1)} collective-permute-done((bf16[3,1,32,128]{3,0,2,1:T(4,128)(2,1)S(1)}, bf16[3,1,32,128]{3,0,2,1:T(4,128)(2,1)S(1)}, u32[]{:S(2)}, u32[]{:S(2)}) %collective-permute-start.21) | collective-permute-done | bytes 24608 | tf_op jit(solution)/shard_map/ppermute | solution.py:19
  257.3 3.4 %collective-permute-start.22 = (bf16[3,6,1,128]{3,0,2,1:T(4,128)(2,1)S(1)}, bf16[3,6,1,128]{3,0,2,1:T(4,128)(2,1)S(1)}, u32[]{:S(2)}, u32[]{:S(2)}) collective-permute-start(bf16[3,6,1,128]{3,0,2,1:T(4,128)(2,1)S(1)} %get-tuple-element.43), channel_id=1, source_target_pairs={{0,2},{1,3},{4,6},{5,7},{8,10},{9,11},{12,14},{13,15},{16,18},{17,... | collective-permute-start | bytes 13832 | tf_op jit(solution)/shard_map/ppermute | solution.py:17
  260.6 1.3 collective-permute-start.23
  262.3 37.5 %psum.95 = f32[3,8,3,3,3]{1,4,3,2,0:T(4,128)} all-reduce(f32[3,8,3,3,3]{1,4,3,2,0:T(4,128)S(1)} %copy.170), channel_id=1, replica_groups=mesh['crops'=2,'xy'=4,'gz'=2,'lab'=2] {'xy','gz'}, use_global_device_ids=true, to_apply=%region_20.21 | all-reduce | flops 648 | bytes 5184 | tf_op jit(solution)/shard_map/psum | solution.py:167
  299.9 0.5 select_maximum_fusion
  305.0 0.4 copy-done.74
  309.0 0.4 copy-done.62
  314.3 0.7 copy.115
  (330 shorter events, 32.3 us)
Async XLA Ops:
  7.2 55.5 %all-reduce.13.cloned.1.call-start = ((), (), s32[]{:S(2)}) async-start(), calls=%async_computation | async-start | bytes 262144 | tf_op jit(solution)/shard_map/psum | solution.py:65
  8.4 14.6 %collective-permute-start.1 = (bf16[8,1,32,128]{3,0,2,1:T(8,128)(2,1)S(1)}, bf16[8,1,32,128]{3,0,2,1:T(8,128)(2,1)S(1)}, u32[]{:S(2)}, u32[]{:S(2)}) collective-permute-start(bf16[8,1,32,128]{3,0,2,1:T(8,128)(2,1)S(1)} %get-tuple-element.39), channel_id=1, source_target_pairs={{4,0},{8,4},{12,8},{5,1},{9,5},{13,9},{6,2},{10,6},{14,10},{7,3},{... | collective-permute-start | bytes 196616 | tf_op jit(solution)/shard_map/ppermute | solution.py:19
  9.7 13.1 %collective-permute-start = (bf16[8,1,32,128]{3,0,2,1:T(8,128)(2,1)S(1)}, bf16[8,1,32,128]{3,0,2,1:T(8,128)(2,1)S(1)}, u32[]{:S(2)}, u32[]{:S(2)}) collective-permute-start(bf16[8,1,32,128]{3,0,2,1:T(8,128)(2,1)S(1)} %get-tuple-element.40), channel_id=1, source_target_pairs={{0,4},{4,8},{8,12},{1,5},{5,9},{9,13},{2,6},{6,10},{10,14},{3,7},{... | collective-permute-start | bytes 196616 | tf_op jit(solution)/shard_map/ppermute | solution.py:17
  16.2 11.6 %collective-permute-start.4 = (bf16[4,1,32,128]{3,2,1,0:T(8,128)(2,1)S(1)}, bf16[4,1,32,128]{3,2,1,0:T(8,128)(2,1)S(1)}, u32[]{:S(2)}, u32[]{:S(2)}) collective-permute-start(bf16[4,1,32,128]{3,2,1,0:T(8,128)(2,1)S(1)} %get-tuple-element.57), channel_id=1, source_target_pairs={{0,4},{4,8},{8,12},{1,5},{5,9},{9,13},{2,6},{6,10},{10,14},{3,7},{... | collective-permute-start | bytes 98312 | tf_op jit(solution)/shard_map/ppermute | solution.py:17
  20.3 7.5 %collective-permute-start.5 = (bf16[4,1,32,128]{3,2,1,0:T(8,128)(2,1)S(1)}, bf16[4,1,32,128]{3,2,1,0:T(8,128)(2,1)S(1)}, u32[]{:S(2)}, u32[]{:S(2)}) collective-permute-start(bf16[4,1,32,128]{3,2,1,0:T(8,128)(2,1)S(1)} %get-tuple-element.58), channel_id=1, source_target_pairs={{4,0},{8,4},{12,8},{5,1},{9,5},{13,9},{6,2},{10,6},{14,10},{7,3},{... | collective-permute-start | bytes 98312 | tf_op jit(solution)/shard_map/ppermute | solution.py:19
  22.5 11.6 %copy-start.47 = (bf16[3,8,1,1,1]{1,4,3,2,0:T(2,128)(2,1)}, bf16[3,8,1,1,1]{1,4,3,2,0:T(2,128)(2,1)S(1)}, u32[]{:S(2)}) copy-start(bf16[3,8,1,1,1]{1,4,3,2,0:T(2,128)(2,1)S(1)} %get-tuple-element.62) | copy-start | bytes 148
  22.5 11.9 %copy-start.45 = (bf16[3,8,1,1,1]{1,4,3,2,0:T(2,128)(2,1)}, bf16[3,8,1,1,1]{1,4,3,2,0:T(2,128)(2,1)S(1)}, u32[]{:S(2)}) copy-start(bf16[3,8,1,1,1]{1,4,3,2,0:T(2,128)(2,1)S(1)} %get-tuple-element.65) | copy-start | bytes 148
  22.5 12.2 %copy-start.43 = (bf16[3,8,1,1,1]{1,4,3,2,0:T(2,128)(2,1)}, bf16[3,8,1,1,1]{1,4,3,2,0:T(2,128)(2,1)S(1)}, u32[]{:S(2)}) copy-start(bf16[3,8,1,1,1]{1,4,3,2,0:T(2,128)(2,1)S(1)} %get-tuple-element.68) | copy-start | bytes 148
  22.6 12.5 %copy-start.41 = (bf16[3,8,1,1,1]{1,4,3,2,0:T(2,128)(2,1)}, bf16[3,8,1,1,1]{1,4,3,2,0:T(2,128)(2,1)S(1)}, u32[]{:S(2)}) copy-start(bf16[3,8,1,1,1]{1,4,3,2,0:T(2,128)(2,1)S(1)} %get-tuple-element.74) | copy-start | bytes 148
  22.6 12.7 %copy-start.39 = (bf16[3,8,1,1,1]{1,4,3,2,0:T(2,128)(2,1)}, bf16[3,8,1,1,1]{1,4,3,2,0:T(2,128)(2,1)S(1)}, u32[]{:S(2)}) copy-start(bf16[3,8,1,1,1]{1,4,3,2,0:T(2,128)(2,1)S(1)} %get-tuple-element.77) | copy-start | bytes 148
  22.6 13.0 %copy-start.37 = (bf16[3,8,1,1,1]{1,4,3,2,0:T(2,128)(2,1)}, bf16[3,8,1,1,1]{1,4,3,2,0:T(2,128)(2,1)S(1)}, u32[]{:S(2)}) copy-start(bf16[3,8,1,1,1]{1,4,3,2,0:T(2,128)(2,1)S(1)} %get-tuple-element.80) | copy-start | bytes 148
  22.6 13.3 %copy-start.35 = (bf16[3,8,1,1,1]{1,4,3,2,0:T(2,128)(2,1)}, bf16[3,8,1,1,1]{1,4,3,2,0:T(2,128)(2,1)S(1)}, u32[]{:S(2)}) copy-start(bf16[3,8,1,1,1]{1,4,3,2,0:T(2,128)(2,1)S(1)} %get-tuple-element.86) | copy-start | bytes 148
  22.6 13.6 %copy-start.33 = (bf16[3,8,1,1,1]{1,4,3,2,0:T(2,128)(2,1)}, bf16[3,8,1,1,1]{1,4,3,2,0:T(2,128)(2,1)S(1)}, u32[]{:S(2)}) copy-start(bf16[3,8,1,1,1]{1,4,3,2,0:T(2,128)(2,1)S(1)} %get-tuple-element.84) | copy-start | bytes 148
  22.6 13.8 %copy-start.79 = (bf16[3,8,1,1,1]{1,4,3,2,0:T(2,128)(2,1)}, bf16[3,8,1,1,1]{1,4,3,2,0:T(2,128)(2,1)S(1)}, u32[]{:S(2)}) copy-start(bf16[3,8,1,1,1]{1,4,3,2,0:T(2,128)(2,1)S(1)} %get-tuple-element.85) | copy-start | bytes 148
  22.6 14.0 %copy-start.77 = (bf16[3,8,1,1,1]{1,4,3,2,0:T(2,128)(2,1)}, bf16[3,8,1,1,1]{1,4,3,2,0:T(2,128)(2,1)S(1)}, u32[]{:S(2)}) copy-start(bf16[3,8,1,1,1]{1,4,3,2,0:T(2,128)(2,1)S(1)} %get-tuple-element.83) | copy-start | bytes 148
  22.6 14.3 %copy-start.75 = (bf16[3,8,1,1,1]{1,4,3,2,0:T(2,128)(2,1)}, bf16[3,8,1,1,1]{1,4,3,2,0:T(2,128)(2,1)S(1)}, u32[]{:S(2)}) copy-start(bf16[3,8,1,1,1]{1,4,3,2,0:T(2,128)(2,1)S(1)} %get-tuple-element.82) | copy-start | bytes 148
  22.6 14.5 %copy-start.31 = (bf16[3,8,1,1,1]{1,4,3,2,0:T(2,128)(2,1)}, bf16[3,8,1,1,1]{1,4,3,2,0:T(2,128)(2,1)S(1)}, u32[]{:S(2)}) copy-start(bf16[3,8,1,1,1]{1,4,3,2,0:T(2,128)(2,1)S(1)} %get-tuple-element.81) | copy-start | bytes 148
  22.6 15.0 %copy-start.73 = (bf16[3,8,1,1,1]{1,4,3,2,0:T(2,128)(2,1)}, bf16[3,8,1,1,1]{1,4,3,2,0:T(2,128)(2,1)S(1)}, u32[]{:S(2)}) copy-start(bf16[3,8,1,1,1]{1,4,3,2,0:T(2,128)(2,1)S(1)} %get-tuple-element.79) | copy-start | bytes 148
  22.7 15.2 %copy-start.71 = (bf16[3,8,1,1,1]{1,4,3,2,0:T(2,128)(2,1)}, bf16[3,8,1,1,1]{1,4,3,2,0:T(2,128)(2,1)S(1)}, u32[]{:S(2)}) copy-start(bf16[3,8,1,1,1]{1,4,3,2,0:T(2,128)(2,1)S(1)} %get-tuple-element.78) | copy-start | bytes 148
  22.7 15.4 %copy-start.69 = (bf16[3,8,1,1,1]{1,4,3,2,0:T(2,128)(2,1)}, bf16[3,8,1,1,1]{1,4,3,2,0:T(2,128)(2,1)S(1)}, u32[]{:S(2)}) copy-start(bf16[3,8,1,1,1]{1,4,3,2,0:T(2,128)(2,1)S(1)} %get-tuple-element.76) | copy-start | bytes 148
  22.7 15.6 %copy-start.67 = (bf16[3,8,1,1,1]{1,4,3,2,0:T(2,128)(2,1)}, bf16[3,8,1,1,1]{1,4,3,2,0:T(2,128)(2,1)S(1)}, u32[]{:S(2)}) copy-start(bf16[3,8,1,1,1]{1,4,3,2,0:T(2,128)(2,1)S(1)} %get-tuple-element.75) | copy-start | bytes 148
  22.7 15.9 %copy-start.65 = (bf16[3,8,1,1,1]{1,4,3,2,0:T(2,128)(2,1)}, bf16[3,8,1,1,1]{1,4,3,2,0:T(2,128)(2,1)S(1)}, u32[]{:S(2)}) copy-start(bf16[3,8,1,1,1]{1,4,3,2,0:T(2,128)(2,1)S(1)} %get-tuple-element.73) | copy-start | bytes 148
  22.7 16.1 %copy-start.63 = (bf16[3,8,1,1,1]{1,4,3,2,0:T(2,128)(2,1)}, bf16[3,8,1,1,1]{1,4,3,2,0:T(2,128)(2,1)S(1)}, u32[]{:S(2)}) copy-start(bf16[3,8,1,1,1]{1,4,3,2,0:T(2,128)(2,1)S(1)} %get-tuple-element.72) | copy-start | bytes 148
  22.7 16.3 %copy-start.61 = (bf16[3,8,1,1,1]{1,4,3,2,0:T(2,128)(2,1)}, bf16[3,8,1,1,1]{1,4,3,2,0:T(2,128)(2,1)S(1)}, u32[]{:S(2)}) copy-start(bf16[3,8,1,1,1]{1,4,3,2,0:T(2,128)(2,1)S(1)} %get-tuple-element.71) | copy-start | bytes 148
  22.7 16.6 %copy-start.59 = (bf16[3,8,1,1,1]{1,4,3,2,0:T(2,128)(2,1)}, bf16[3,8,1,1,1]{1,4,3,2,0:T(2,128)(2,1)S(1)}, u32[]{:S(2)}) copy-start(bf16[3,8,1,1,1]{1,4,3,2,0:T(2,128)(2,1)S(1)} %get-tuple-element.70) | copy-start | bytes 148
  22.7 16.8 %copy-start.57 = (bf16[3,8,1,1,1]{1,4,3,2,0:T(2,128)(2,1)}, bf16[3,8,1,1,1]{1,4,3,2,0:T(2,128)(2,1)S(1)}, u32[]{:S(2)}) copy-start(bf16[3,8,1,1,1]{1,4,3,2,0:T(2,128)(2,1)S(1)} %get-tuple-element.69) | copy-start | bytes 148
  22.7 17.1 %copy-start.55 = (bf16[3,8,1,1,1]{1,4,3,2,0:T(2,128)(2,1)}, bf16[3,8,1,1,1]{1,4,3,2,0:T(2,128)(2,1)S(1)}, u32[]{:S(2)}) copy-start(bf16[3,8,1,1,1]{1,4,3,2,0:T(2,128)(2,1)S(1)} %get-tuple-element.67) | copy-start | bytes 148
  22.7 17.3 %copy-start.53 = (bf16[3,8,1,1,1]{1,4,3,2,0:T(2,128)(2,1)}, bf16[3,8,1,1,1]{1,4,3,2,0:T(2,128)(2,1)S(1)}, u32[]{:S(2)}) copy-start(bf16[3,8,1,1,1]{1,4,3,2,0:T(2,128)(2,1)S(1)} %get-tuple-element.66) | copy-start | bytes 148
  22.8 17.5 %copy-start.51 = (bf16[3,8,1,1,1]{1,4,3,2,0:T(2,128)(2,1)}, bf16[3,8,1,1,1]{1,4,3,2,0:T(2,128)(2,1)S(1)}, u32[]{:S(2)}) copy-start(bf16[3,8,1,1,1]{1,4,3,2,0:T(2,128)(2,1)S(1)} %get-tuple-element.64) | copy-start | bytes 148
  22.8 18.3 %copy-start.49 = (bf16[3,8,1,1,1]{1,4,3,2,0:T(2,128)(2,1)}, bf16[3,8,1,1,1]{1,4,3,2,0:T(2,128)(2,1)S(1)}, u32[]{:S(2)}) copy-start(bf16[3,8,1,1,1]{1,4,3,2,0:T(2,128)(2,1)S(1)} %get-tuple-element.61) | copy-start | bytes 148
  22.8 10.9 %copy-start.26 = (bf16[8,1,32,128]{3,0,2,1:T(8,128)(2,1)}, bf16[8,1,32,128]{3,0,2,1:T(8,128)(2,1)S(1)}, u32[]{:S(2)}) copy-start(bf16[8,1,32,128]{3,0,2,1:T(8,128)(2,1)S(1)} %collective-permute-done) | copy-start | bytes 196612
  23.0 10.7 %copy-start.23 = (bf16[8,1,32,128]{3,0,2,1:T(8,128)(2,1)}, bf16[8,1,32,128]{3,0,2,1:T(8,128)(2,1)S(1)}, u32[]{:S(2)}) copy-start(bf16[8,1,32,128]{3,0,2,1:T(8,128)(2,1)S(1)} %collective-permute-done.1) | copy-start | bytes 196612
  23.1 10.6 %collective-permute-start.2 = (bf16[8,6,1,128]{3,0,2,1:T(8,128)(2,1)S(1)}, bf16[8,6,1,128]{3,0,2,1:T(8,128)(2,1)S(1)}, u32[]{:S(2)}, u32[]{:S(2)}) collective-permute-start(bf16[8,6,1,128]{3,0,2,1:T(8,128)(2,1)S(1)} %get-tuple-element.28), channel_id=1, source_target_pairs={{0,2},{1,3},{4,6},{5,7},{8,10},{9,11},{12,14},{13,15},{16,18},{17,... | collective-permute-start | bytes 36872 | tf_op jit(solution)/shard_map/ppermute | solution.py:17
  26.5 7.2 %collective-permute-start.3 = (bf16[8,6,1,128]{3,0,2,1:T(8,128)(2,1)S(1)}, bf16[8,6,1,128]{3,0,2,1:T(8,128)(2,1)S(1)}, u32[]{:S(2)}, u32[]{:S(2)}) collective-permute-start(bf16[8,6,1,128]{3,0,2,1:T(8,128)(2,1)S(1)} %get-tuple-element.29), channel_id=1, source_target_pairs={{2,0},{3,1},{6,4},{7,5},{10,8},{11,9},{14,12},{15,13},{18,16},{19,... | collective-permute-start | bytes 36872 | tf_op jit(solution)/shard_map/ppermute | solution.py:19
  27.8 14.4 %collective-permute-start.6 = (bf16[4,6,1,128]{3,2,1,0:T(2,128)(2,1)S(1)}, bf16[4,6,1,128]{3,2,1,0:T(2,128)(2,1)S(1)}, u32[]{:S(2)}, u32[]{:S(2)}) collective-permute-start(bf16[4,6,1,128]{3,2,1,0:T(2,128)(2,1)S(1)} %get-tuple-element.49), channel_id=1, source_target_pairs={{0,2},{1,3},{4,6},{5,7},{8,10},{9,11},{12,14},{13,15},{16,18},{17,... | collective-permute-start | bytes 18440 | tf_op jit(solution)/shard_map/ppermute | solution.py:17
  32.4 9.8 %collective-permute-start.7 = (bf16[4,6,1,128]{3,2,1,0:T(2,128)(2,1)S(1)}, bf16[4,6,1,128]{3,2,1,0:T(2,128)(2,1)S(1)}, u32[]{:S(2)}, u32[]{:S(2)}) collective-permute-start(bf16[4,6,1,128]{3,2,1,0:T(2,128)(2,1)S(1)} %get-tuple-element.50), channel_id=1, source_target_pairs={{2,0},{3,1},{6,4},{7,5},{10,8},{11,9},{14,12},{15,13},{18,16},{19,... | collective-permute-start | bytes 18440 | tf_op jit(solution)/shard_map/ppermute | solution.py:19
  42.2 196.1 %all-reduce.15.cloned.1.call-start = ((), (), s32[]{:S(2)}) async-start(), calls=%async_computation.1 | async-start | bytes 524288 | tf_op jit(solution)/shard_map/psum | solution.py:139
  64.4 7.6 %collective-permute-start.9 = (f32[4,1,128]{2,0,1:T(4,128)S(1)}, f32[4,1,128]{2,0,1:T(4,128)S(1)}, u32[]{:S(2)}, u32[]{:S(2)}) collective-permute-start(f32[4,1,128]{2,0,1:T(4,128)S(1)} %bitcast.468), channel_id=1, source_target_pairs={{0,2},{1,3},{4,6},{5,7},{8,10},{9,11},{12,14},{13,15},{16,18},{17,... | collective-permute-start | bytes 6152 | tf_op jit(solution)/shard_map/ppermute | solution.py:29
  68.4 4.8 %collective-permute-start.8 = (f32[1,32,128]{2,1,0:T(8,128)S(1)}, f32[1,32,128]{2,1,0:T(8,128)S(1)}, u32[]{:S(2)}, u32[]{:S(2)}) collective-permute-start(f32[1,32,128]{2,1,0:T(8,128)S(1)} %bitcast.466), channel_id=1, source_target_pairs={{0,4},{4,8},{8,12},{1,5},{5,9},{9,13},{2,6},{6,10},{10,14},{3,7},{... | collective-permute-start | bytes 49160 | tf_op jit(solution)/shard_map/ppermute | solution.py:29
  107.8 16.1 %copy-start.83 = (f32[4]{0:T(128)}, f32[4]{0:T(128)S(1)}, u32[]{:S(2)}) copy-start(f32[4]{0:T(128)S(1)} %div.24) | copy-start | bytes 52
  123.9 3.5 %collective-permute-start.10 = (bf16[4,1,32,128]{3,2,1,0:T(8,128)(2,1)S(1)}, bf16[4,1,32,128]{3,2,1,0:T(8,128)(2,1)S(1)}, u32[]{:S(2)}, u32[]{:S(2)}) collective-permute-start(bf16[4,1,32,128]{3,2,1,0:T(8,128)(2,1)S(1)} %get-tuple-element.55), channel_id=1, source_target_pairs={{0,4},{4,8},{8,12},{1,5},{5,9},{9,13},{2,6},{6,10},{10,14},{3,7},{... | collective-permute-start | bytes 98312 | tf_op jit(solution)/shard_map/ppermute | solution.py:17
  125.8 5.8 %collective-permute-start.11 = (bf16[4,1,32,128]{3,2,1,0:T(8,128)(2,1)S(1)}, bf16[4,1,32,128]{3,2,1,0:T(8,128)(2,1)S(1)}, u32[]{:S(2)}, u32[]{:S(2)}) collective-permute-start(bf16[4,1,32,128]{3,2,1,0:T(8,128)(2,1)S(1)} %get-tuple-element.56), channel_id=1, source_target_pairs={{4,0},{8,4},{12,8},{5,1},{9,5},{13,9},{6,2},{10,6},{14,10},{7,3},{... | collective-permute-start | bytes 98312 | tf_op jit(solution)/shard_map/ppermute | solution.py:19
  131.7 3.9 %collective-permute-start.12 = (bf16[4,6,1,128]{3,2,1,0:T(2,128)(2,1)S(1)}, bf16[4,6,1,128]{3,2,1,0:T(2,128)(2,1)S(1)}, u32[]{:S(2)}, u32[]{:S(2)}) collective-permute-start(bf16[4,6,1,128]{3,2,1,0:T(2,128)(2,1)S(1)} %get-tuple-element.47), channel_id=1, source_target_pairs={{0,2},{1,3},{4,6},{5,7},{8,10},{9,11},{12,14},{13,15},{16,18},{17,... | collective-permute-start | bytes 18440 | tf_op jit(solution)/shard_map/ppermute | solution.py:17
  134.0 5.6 %collective-permute-start.13 = (bf16[4,6,1,128]{3,2,1,0:T(2,128)(2,1)S(1)}, bf16[4,6,1,128]{3,2,1,0:T(2,128)(2,1)S(1)}, u32[]{:S(2)}, u32[]{:S(2)}) collective-permute-start(bf16[4,6,1,128]{3,2,1,0:T(2,128)(2,1)S(1)} %get-tuple-element.48), channel_id=1, source_target_pairs={{2,0},{3,1},{6,4},{7,5},{10,8},{11,9},{14,12},{15,13},{18,16},{19,... | collective-permute-start | bytes 18440 | tf_op jit(solution)/shard_map/ppermute | solution.py:19
  158.6 14.0 %copy-start.81 = (f32[4]{0:T(128)}, f32[4]{0:T(128)S(1)}, u32[]{:S(2)}) copy-start(f32[4]{0:T(128)S(1)} %div.26) | copy-start | bytes 52
  174.6 4.9 %collective-permute-start.14 = (bf16[4,1,32,128]{3,2,1,0:T(8,128)(2,1)S(1)}, bf16[4,1,32,128]{3,2,1,0:T(8,128)(2,1)S(1)}, u32[]{:S(2)}, u32[]{:S(2)}) collective-permute-start(bf16[4,1,32,128]{3,2,1,0:T(8,128)(2,1)S(1)} %get-tuple-element.53), channel_id=1, source_target_pairs={{0,4},{4,8},{8,12},{1,5},{5,9},{9,13},{2,6},{6,10},{10,14},{3,7},{... | collective-permute-start | bytes 98312 | tf_op jit(solution)/shard_map/ppermute | solution.py:17
  178.0 5.8 %collective-permute-start.15 = (bf16[4,1,32,128]{3,2,1,0:T(8,128)(2,1)S(1)}, bf16[4,1,32,128]{3,2,1,0:T(8,128)(2,1)S(1)}, u32[]{:S(2)}, u32[]{:S(2)}) collective-permute-start(bf16[4,1,32,128]{3,2,1,0:T(8,128)(2,1)S(1)} %get-tuple-element.54), channel_id=1, source_target_pairs={{4,0},{8,4},{12,8},{5,1},{9,5},{13,9},{6,2},{10,6},{14,10},{7,3},{... | collective-permute-start | bytes 98312 | tf_op jit(solution)/shard_map/ppermute | solution.py:19
  183.8 5.4 %collective-permute-start.16 = (bf16[4,6,1,128]{3,2,1,0:T(2,128)(2,1)S(1)}, bf16[4,6,1,128]{3,2,1,0:T(2,128)(2,1)S(1)}, u32[]{:S(2)}, u32[]{:S(2)}) collective-permute-start(bf16[4,6,1,128]{3,2,1,0:T(2,128)(2,1)S(1)} %get-tuple-element.45), channel_id=1, source_target_pairs={{0,2},{1,3},{4,6},{5,7},{8,10},{9,11},{12,14},{13,15},{16,18},{17,... | collective-permute-start | bytes 18440 | tf_op jit(solution)/shard_map/ppermute | solution.py:17
  187.7 5.6 %collective-permute-start.17 = (bf16[4,6,1,128]{3,2,1,0:T(2,128)(2,1)S(1)}, bf16[4,6,1,128]{3,2,1,0:T(2,128)(2,1)S(1)}, u32[]{:S(2)}, u32[]{:S(2)}) collective-permute-start(bf16[4,6,1,128]{3,2,1,0:T(2,128)(2,1)S(1)} %get-tuple-element.46), channel_id=1, source_target_pairs={{2,0},{3,1},{6,4},{7,5},{10,8},{11,9},{14,12},{15,13},{18,16},{19,... | collective-permute-start | bytes 18440 | tf_op jit(solution)/shard_map/ppermute | solution.py:19
  193.5 17.5 %copy-start.87 = (f32[4]{0:T(128)S(1)}, f32[4]{0:T(128)}, u32[]{:S(2)}) copy-start(f32[4]{0:T(128)} %copy-done.86) | copy-start | bytes 52
  193.5 17.5 %copy-start.82 = (f32[4]{0:T(128)S(1)}, f32[4]{0:T(128)}, u32[]{:S(2)}) copy-start(f32[4]{0:T(128)} %copy-done.81) | copy-start | bytes 52
  193.5 17.5 %copy-start.84 = (f32[4]{0:T(128)S(1)}, f32[4]{0:T(128)}, u32[]{:S(2)}) copy-start(f32[4]{0:T(128)} %copy-done.83) | copy-start | bytes 52
  211.5 7.7 %collective-permute-start.19 = (f32[8,4,1,128]{3,2,1,0:T(1,128)S(1)}, f32[8,4,1,128]{3,2,1,0:T(1,128)S(1)}, u32[]{:S(2)}, u32[]{:S(2)}) collective-permute-start(f32[8,4,1,128]{3,2,1,0:T(1,128)S(1)} %fusion.176), channel_id=1, source_target_pairs={{2,0},{3,1},{6,4},{7,5},{10,8},{11,9},{14,12},{15,13},{18,16},{19,... | collective-permute-start | bytes 49160 | tf_op jit(solution)/shard_map/ppermute | solution.py:29
  212.9 6.2 %collective-permute-start.18 = (bf16[8,1,32,128]{3,2,1,0:T(8,128)(2,1)S(1)}, bf16[8,1,32,128]{3,2,1,0:T(8,128)(2,1)S(1)}, u32[]{:S(2)}, u32[]{:S(2)}) collective-permute-start(bf16[8,1,32,128]{3,2,1,0:T(8,128)(2,1)S(1)} %fusion.141), channel_id=1, source_target_pairs={{4,0},{8,4},{12,8},{5,1},{9,5},{13,9},{6,2},{10,6},{14,10},{7,3},{... | collective-permute-start | bytes 196616 | tf_op jit(solution)/shard_map/ppermute | solution.py:29
  219.5 18.8 %copy-start.15 = (pred[1,4,32,128]{3,0,2,1:T(4,128)(4,1)S(1)}, pred[1,4,32,128]{3,0,2,1:T(4,128)(4,1)}, u32[]{:S(2)}) copy-start(pred[1,4,32,128]{3,0,2,1:T(4,128)(4,1)} %copy-done.14) | copy-start | bytes 49156
  219.5 18.8 %copy-start.17 = (pred[1,4,32,128]{3,0,2,1:T(4,128)(4,1)S(1)}, pred[1,4,32,128]{3,0,2,1:T(4,128)(4,1)}, u32[]{:S(2)}) copy-start(pred[1,4,32,128]{3,0,2,1:T(4,128)(4,1)} %copy-done.16) | copy-start | bytes 49156
  219.5 18.8 %copy-start.19 = (pred[1,4,32,128]{3,0,2,1:T(4,128)(4,1)S(1)}, pred[1,4,32,128]{3,0,2,1:T(4,128)(4,1)}, u32[]{:S(2)}) copy-start(pred[1,4,32,128]{3,0,2,1:T(4,128)(4,1)} %copy-done.18) | copy-start | bytes 49156
  219.5 18.8 %copy-start.20 = (bf16[3,4,32,128]{3,0,2,1:T(4,128)(2,1)S(1)}, bf16[3,4,32,128]{3,0,2,1:T(4,128)(2,1)}, u32[]{:S(2)}) copy-start(bf16[3,4,32,128]{3,0,2,1:T(4,128)(2,1)} %all-reduce.13.cloned.1.call-done) | copy-start | bytes 294916
  247.8 5.3 %collective-permute-start.20 = (bf16[3,1,32,128]{3,0,2,1:T(4,128)(2,1)S(1)}, bf16[3,1,32,128]{3,0,2,1:T(4,128)(2,1)S(1)}, u32[]{:S(2)}, u32[]{:S(2)}) collective-permute-start(bf16[3,1,32,128]{3,0,2,1:T(4,128)(2,1)S(1)} %get-tuple-element.51), channel_id=1, source_target_pairs={{0,4},{4,8},{8,12},{1,5},{5,9},{9,13},{2,6},{6,10},{10,14},{3,7},{... | collective-permute-start | bytes 73736 | tf_op jit(solution)/shard_map/ppermute | solution.py:17
  251.4 5.8 %collective-permute-start.21 = (bf16[3,1,32,128]{3,0,2,1:T(4,128)(2,1)S(1)}, bf16[3,1,32,128]{3,0,2,1:T(4,128)(2,1)S(1)}, u32[]{:S(2)}, u32[]{:S(2)}) collective-permute-start(bf16[3,1,32,128]{3,0,2,1:T(4,128)(2,1)S(1)} %get-tuple-element.52), channel_id=1, source_target_pairs={{4,0},{8,4},{12,8},{5,1},{9,5},{13,9},{6,2},{10,6},{14,10},{7,3},{... | collective-permute-start | bytes 73736 | tf_op jit(solution)/shard_map/ppermute | solution.py:19
  253.0 47.3 %copy-start.48 = (bf16[3,8,1,1,1]{1,4,3,2,0:T(2,128)(2,1)S(1)}, bf16[3,8,1,1,1]{1,4,3,2,0:T(2,128)(2,1)}, u32[]{:S(2)}) copy-start(bf16[3,8,1,1,1]{1,4,3,2,0:T(2,128)(2,1)} %copy-done.47) | copy-start | bytes 148
  257.3 42.6 %collective-permute-start.22 = (bf16[3,6,1,128]{3,0,2,1:T(4,128)(2,1)S(1)}, bf16[3,6,1,128]{3,0,2,1:T(4,128)(2,1)S(1)}, u32[]{:S(2)}, u32[]{:S(2)}) collective-permute-start(bf16[3,6,1,128]{3,0,2,1:T(4,128)(2,1)S(1)} %get-tuple-element.43), channel_id=1, source_target_pairs={{0,2},{1,3},{4,6},{5,7},{8,10},{9,11},{12,14},{13,15},{16,18},{17,... | collective-permute-start | bytes 13832 | tf_op jit(solution)/shard_map/ppermute | solution.py:17
  260.6 39.2 %collective-permute-start.23 = (bf16[3,6,1,128]{3,0,2,1:T(4,128)(2,1)S(1)}, bf16[3,6,1,128]{3,0,2,1:T(4,128)(2,1)S(1)}, u32[]{:S(2)}, u32[]{:S(2)}) collective-permute-start(bf16[3,6,1,128]{3,0,2,1:T(4,128)(2,1)S(1)} %get-tuple-element.44), channel_id=1, source_target_pairs={{2,0},{3,1},{6,4},{7,5},{10,8},{11,9},{14,12},{15,13},{18,16},{19,... | collective-permute-start | bytes 13832 | tf_op jit(solution)/shard_map/ppermute | solution.py:19
  262.3 38.4 %copy-start.46 = (bf16[3,8,1,1,1]{1,4,3,2,0:T(2,128)(2,1)S(1)}, bf16[3,8,1,1,1]{1,4,3,2,0:T(2,128)(2,1)}, u32[]{:S(2)}) copy-start(bf16[3,8,1,1,1]{1,4,3,2,0:T(2,128)(2,1)} %copy-done.45) | copy-start | bytes 148
  (50 other events, 153.8 us)
Sparse Core Ops, SparseCore 0:
  42.3 20.3 all-reduce.12
  220.7 17.5 all-reduce.14
